TPU v7x, 32 devices: a whole 2x2x4 slice. The times are simulated.
32 devices in a mesh: group: 2 (over y), mid: 4 (over z), freq: 2 (over x), off: 2 (over core).
Axes of the slice: x: 2, y: 2, z: 4, core: 2. Of those that a mesh axis runs over, the one named last changes fastest.
Arguments:
- traces: bfloat16 [2, 1024, 1024], P('off', ('group', 'mid', 'freq')), parts along dimension 1, may hold values from -6 to 6
- time_filter: bfloat16 [1024, 1024], replicated, may hold values from -0.1875 to 0.1875
- midpoint_of: int32 [2, 1024], P('off', 'group'), parts along dimension 1, may hold values from 0 to 7, as said below
- offset_of: int32 [2, 1024], P('off', 'group'), parts along dimension 1, may hold values from 0 to 127, as said below
- shrink_level: float32 [512], P('freq'), may hold values from 0.2 to 2
Outputs:
- primaries: bfloat16 [2, 1024, 1024], P('off', ('group', 'mid', 'freq')), parts along dimension 1
There are 2 independent parts, one for each index of `group`. A program takes and returns all parts, laid end to end along the dimension named above; an argument that names none is the same for every part. Nothing has to cross between parts.
Inputs may be any that keep to these rules, and one draw needn't show every extreme that they name: `midpoint_of`: together with offset_of, every (midpoint, offset) pair occurs exactly once in a part; the traces of one device (a block of 64 along the second dimension) go to midpoint owners (midpoint // 2) in counts of 32 for a quarter of the owners, 16 for another quarter and 8 for the rest, so at most 32 traces from one device reach one owner. `offset_of`: traces at first index o have offsets in o * 64 up to (o + 1) * 64 - 1.
All inputs are finite; a program needn't handle non-finite values.
Results may differ from a plain program's by a relative error of at most 0.0076.
Values may be sent and summed in bfloat16 or wider, within the bound.
A program may use at most 64 MiB of HBM per device.

v0:
```python
import math

import jax
import jax.numpy as jnp
from jax import lax
from jax.sharding import PartitionSpec as P

NOFF = 128
NP = 128


two_pi = 2.0 * math.pi
radon_period = 4096


def with_halo(cells, sides, width):
    for axis, dim in sides:
        count = lax.axis_size(axis)
        ends = count - 1
        head = lax.slice_in_dim(cells, 0, width, axis=dim)
        tail = lax.slice_in_dim(cells, cells.shape[dim] - width, cells.shape[dim], axis=dim)
        cells = jnp.concatenate(
            [
                lax.ppermute(tail, axis, [(i, (i + 1) % count) for i in range(ends)]),
                cells,
                lax.ppermute(head, axis, [((i + 1) % count, i) for i in range(ends)]),
            ],
            axis=dim,
        )
    return cells


def dft_table(n_time, n_bands, band_size):
    sample = jnp.arange(n_time, dtype=jnp.int32)[:, None, None]
    freq_index = (
        jnp.arange(n_bands, dtype=jnp.int32)[None, :, None] * band_size
        + jnp.arange(band_size, dtype=jnp.int32)[None, None, :]
    )
    angle = two_pi * (sample * freq_index % n_time).astype(jnp.float32) / n_time
    scale_f = 1.0 / math.sqrt(n_time)
    cosine = (jnp.cos(angle) * scale_f).astype(jnp.bfloat16)
    sine = (-jnp.sin(angle) * scale_f).astype(jnp.bfloat16)
    return jnp.stack([cosine, sine], axis=2).reshape(n_time, n_bands * 2 * band_size)


def radon_table(freq_first, band_size, off_first, noff_dev):
    freq_index = freq_first + jnp.arange(band_size, dtype=jnp.int32)[:, None, None]
    offset_index = off_first + jnp.arange(noff_dev, dtype=jnp.int32)[None, :, None]
    slowness = jnp.arange(NP, dtype=jnp.int32)[None, None, :]
    turns = (
        freq_index
        * slowness
        % radon_period
        * (offset_index * offset_index % radon_period)
        % radon_period
    )
    angle = two_pi * turns.astype(jnp.float32) / radon_period
    scale_r = 1.0 / math.sqrt(NOFF)
    cosine = (jnp.cos(angle) * scale_r).astype(jnp.bfloat16)
    sine = (jnp.sin(angle) * scale_r).astype(jnp.bfloat16)
    first = jnp.stack([cosine, sine], axis=2)
    second = jnp.stack([-sine, cosine], axis=2)
    return jnp.stack([first, second], axis=1)


def shrink(model, levels):
    power = model[:, :, 0, :] * model[:, :, 0, :] + model[:, :, 1, :] * model[:, :, 1, :]
    mask_p = (jnp.arange(NP) >= NP // 4).astype(jnp.float32)
    level_sq = levels[:, None, None] * levels[:, None, None]
    factor = power / (power + level_sq) * mask_p
    return (model * factor[:, :, None, :]).astype(jnp.bfloat16)


def on_device(traces, time_filter, midpoint_of, offset_of, shrink_level):
    n_mid = lax.axis_size("mid")
    n_freq = lax.axis_size("freq")
    me_mid = lax.axis_index("mid")
    me_freq = lax.axis_index("freq")
    me_off = lax.axis_index("off")
    tr_dev = traces.shape[1]
    n_time = traces.shape[2]
    band_size = shrink_level.shape[0]
    noff_dev = NOFF // lax.axis_size("off")
    cmp_dev = n_freq * tr_dev // noff_dev
    capacity = 2 * tr_dev // n_mid
    n_send = n_mid * n_freq
    n_cells = cmp_dev * noff_dev
    n_slots = n_send * capacity
    row_width = 2 * band_size
    filtered = jnp.dot(traces[0], time_filter, preferred_element_type=jnp.float32).astype(
        jnp.bfloat16
    )
    table = dft_table(n_time, n_freq, band_size)
    spectra = jnp.dot(filtered, table, preferred_element_type=jnp.float32).astype(jnp.bfloat16)
    mids_all = midpoint_of[0].reshape(n_send, tr_dev)
    offs_all = offset_of[0].reshape(n_send, tr_dev)
    own_row = mids_all[me_mid * n_freq + me_freq]
    own_offs = offs_all[me_mid * n_freq + me_freq]
    own_dest = own_row // cmp_dev
    own_cell = own_row % cmp_dev * noff_dev + own_offs % noff_dev
    onehot = (own_dest[:, None] == jnp.arange(n_mid, dtype=jnp.int32)[None, :]).astype(jnp.int32)
    own_rank = jnp.sum(jnp.cumsum(onehot, axis=0) * onehot, axis=1) - 1
    own_slot = own_dest * capacity + own_rank
    slot_hits = (
        jnp.arange(n_mid * capacity, dtype=jnp.int32)[:, None] == own_slot[None, :]
    ).astype(jnp.int32)
    send_hot = slot_hits.astype(jnp.bfloat16)
    slot_cell = (
        jnp.sum(slot_hits * own_cell[None, :], axis=1) + (1 - jnp.sum(slot_hits, axis=1)) * n_cells
    )
    outgoing = jnp.dot(send_hot, spectra, preferred_element_type=jnp.float32).astype(jnp.bfloat16)
    blocks = outgoing.reshape(n_mid, capacity, n_freq, row_width)
    cell_ids = jnp.broadcast_to(slot_cell.reshape(n_mid, capacity, 1), (n_mid, capacity, n_freq))
    flat_blocks = jnp.transpose(blocks, (0, 2, 1, 3)).reshape(n_slots, row_width)
    flat_cells = jnp.transpose(cell_ids, (0, 2, 1)).reshape(n_slots)
    got_rows, got_cells = (
        lax.all_to_all(flat_blocks, ("mid", "freq"), split_axis=0, concat_axis=0, tiled=True),
        lax.all_to_all(flat_cells, ("mid", "freq"), split_axis=0, concat_axis=0, tiled=True),
    )
    recv_hot = (jnp.arange(n_cells, dtype=jnp.int32)[:, None] == got_cells[None, :]).astype(
        jnp.bfloat16
    )
    grid = (
        jnp.dot(recv_hot, got_rows, preferred_element_type=jnp.float32)
        .astype(jnp.bfloat16)
        .reshape(cmp_dev, noff_dev, 2, band_size)
    )
    padded = with_halo(grid, (("mid", 0),), 1)
    smooth = (
        (
            padded[:-2].astype(jnp.float32)
            + 2.0 * padded[1:-1].astype(jnp.float32)
            + padded[2:].astype(jnp.float32)
        )
        * 0.25
    ).astype(jnp.bfloat16)
    weights = radon_table(me_freq * band_size, band_size, me_off * noff_dev, noff_dev)
    model_part = jnp.einsum("chrk,krhsp->kcsp", smooth, weights, preferred_element_type=jnp.float32)
    model_half = lax.psum_scatter(model_part, "off", scatter_dimension=1, tiled=True)
    kept_half = shrink(model_half, shrink_level)
    kept = lax.all_gather(kept_half, "off", axis=1, tiled=True)
    multiples = jnp.einsum("kcsp,krhsp->chrk", kept, weights, preferred_element_type=jnp.float32)
    cleaned = (grid.astype(jnp.float32) - multiples).astype(jnp.bfloat16)
    back_rows = lax.dot_general(
        recv_hot,
        cleaned.reshape(n_cells, row_width),
        (((0,), (0,)), ((), ())),
        preferred_element_type=jnp.float32,
    ).astype(jnp.bfloat16)
    returned = lax.all_to_all(back_rows, ("mid", "freq"), split_axis=0, concat_axis=0, tiled=True)
    ordered = jnp.transpose(
        returned.reshape(n_mid, n_freq, capacity, row_width), (0, 2, 1, 3)
    ).reshape(n_mid * capacity, n_freq * row_width)
    back_spec = lax.dot_general(
        send_hot, ordered, (((0,), (0,)), ((), ())), preferred_element_type=jnp.float32
    ).astype(jnp.bfloat16)
    total = lax.dot_general(
        back_spec, table, (((1,), (1,)), ((), ())), preferred_element_type=jnp.float32
    )
    return (2.0 * total).astype(jnp.bfloat16)[None]


def solution(mesh):
    return jax.shard_map(
        on_device,
        mesh=mesh,
        in_specs=(
            P("off", ("group", "mid", "freq"), None),
            P(),
            P("off", "group"),
            P("off", "group"),
            P("freq"),
        ),
        out_specs=P("off", ("group", "mid", "freq"), None),
        check_vma=False,
    )
```

profile of v0, /device:TPU:0, one launch (start us, length us, event | category | flops | bytes accessed | tf_op | source)
XLA Modules:
  0.0 192.8 jit_solution(2193440611483586898)
XLA Ops:
  7.1 1.5 reduce.9
  8.7 1.4 reduce.10
  10.7 0.6 transpose.30
  11.3 7.3 %all-to-all-start = ((s32[8,32,1]{1,2,0:T(1,128)}), s32[8,32,1]{1,2,0:T(1,128)S(1)}, u32[]{:S(2)}, u32[]{:S(2)}) async-start(s32[8,32,1]{1,2,0:T(1,128)} %bitcast.4), calls=%async_computation | async-start | bytes 8192 | tf_op jit(solution)/shard_map/all_to_all | solution.py:118
  18.7 9.8 %multiply_convert_fusion.3 = (bf16[1024,2,1,256]{0,3,2,1:T(8,128)(2,1)S(1)}, bf16[1024,2,1,256]{0,3,2,1:T(8,128)(2,1)}) fusion(s32[2,256]{1,0:T(2,128)S(1)} %iota_add_fusion), kind=kLoop, calls=%fused_computation.23 | loop fusion | flops 9961472 | bytes 2099200 | tf_op jit(solution)/shard_map/convert_element_type | solution.py:41
  28.6 2.8 %pad_maximum_fusion.3 = bf16[1024,2,2,256]{0,3,2,1:T(8,128)(2,1)} fusion(bf16[1024,2,1,256]{0,3,2,1:T(8,128)(2,1)} %get-tuple-element.16, bf16[1024,2,1,256]{0,3,2,1:T(8,128)(2,1)S(1)} %get-tuple-element.15), kind=kLoop, calls=%fused_computation.21 | loop fusion | flops 1048576 | bytes 4194304 | tf_op jit(solution)/shard_map/stack | solution.py:43
  31.4 35.3 %multiply_convert_fusion = (bf16[256,64,1,128]{3,1,2,0:T(8,128)(2,1)}, bf16[256,64,1,128]{3,1,2,0:T(8,128)(2,1)}) fusion(s32[64]{0:T(128)S(1)} %get-tuple-element.17, s32[256,128]{1,0:T(8,128)S(1)} %add_select_fusion.2), kind=kLoop, calls=%fused_computation.13 | loop fusion | flops 37748736 | bytes 8519936 | tf_op jit(solution)/shard_map/convert_element_type | solution.py:60
  67.2 2.5 %convolution_convert_fusion.1 = bf16[128,1024]{1,0:T(8,128)(2,1)S(1)} fusion(bf16[64,1024]{1,0:T(8,128)(2,1)S(1)} %convolution_convert_fusion.5, bf16[1024,1024]{0,1:T(8,128)(2,1)} %bitcast.70, s32[64]{0:T(128)S(1)} %get-tuple-element.14), kind=kOutput, calls=%fused_computation.30 | convolution fusion | flops 151216128 | bytes 2490624 | tf_op jit(solution)/shard_map/dot_general | solution.py:111
  69.9 0.7 copy.95
  70.6 6.0 %all-to-all-start.1 = ((bf16[8,32,512]{2,1,0:T(8,128)(2,1)}), bf16[8,32,512]{2,1,0:T(8,128)(2,1)S(1)}, u32[]{:S(2)}, u32[]{:S(2)}) async-start(bf16[8,32,512]{2,1,0:T(8,128)(2,1)} %bitcast.8), calls=%async_computation.1 | async-start | bytes 524288 | tf_op jit(solution)/shard_map/all_to_all | solution.py:117
  76.8 32.3 %fusion.15 = bf16[256,64,1,128]{3,1,2,0:T(8,128)(2,1)} fusion(s32[64]{0:T(128)S(1)} %get-tuple-element.17, s32[256,128]{1,0:T(8,128)S(1)} %add_select_fusion.2), kind=kLoop, calls=%fused_computation.38 | loop fusion | flops 39845888 | bytes 4325632 | tf_op jit(solution)/shard_map/neg | solution.py:62
  109.2 0.7 reduce.11
  110.2 1.3 collective-permute-start.1
  111.6 4.5 %collective-permute-start = (bf16[1,64,2,256]{3,1,2,0:T(8,128)(2,1)S(1)}, bf16[1,64,2,256]{3,1,2,0:T(8,128)(2,1)S(1)}, u32[]{:S(2)}, u32[]{:S(2)}) collective-permute-start(bf16[1,64,2,256]{3,1,2,0:T(8,128)(2,1)S(1)} %copy.98), channel_id=1, source_target_pairs={{0,4},{4,8},{8,12},{1,5},{5,9},{9,13},{2,6},{6,10},{10,14},{3,7},{... | collective-permute-start | bytes 196616 | tf_op jit(solution)/shard_map/ppermute | solution.py:24
  116.1 13.3 %maximum_bitcast_fusion = (bf16[256,1,64,2,128]{4,2,1,3,0:T(8,128)(2,1)}, bf16[256,1,64,2,128]{4,2,1,3,0:T(8,128)(2,1)}) fusion(bf16[256,64,1,128]{3,1,2,0:T(8,128)(2,1)} %get-tuple-element.9, bf16[256,64,1,128]{3,1,2,0:T(8,128)(2,1)} %get-tuple-element.10, bf16[256,64,1,128]{3,1,2,0:T(8,128)(2,1)} %fusion.15), kind=kLoop, calls=%fused_computation.11 | loop fusion | flops 8388608 | bytes 29360128 | tf_op jit(solution)/shard_map/stack | solution.py:63
  129.8 7.2 %fusion.11 = f32[256,2,2,128]{3,1,2,0:T(2,128)S(1)} fusion(bf16[2,64,2,256,1]{1,0,2,4,3:T(2,128)(2,1)S(1)} %copy.109, bf16[256,1,64,2,128]{4,2,1,3,0:T(8,128)(2,1)} %get-tuple-element.8, bf16[256,1,64,2,128]{4,2,1,3,0:T(8,128)(2,1)} %get-tuple-element.7), kind=kOutput, calls=%fused_computation.27 | convolution fusion | flops 67108864 | bytes 17432576 | tf_op jit(solution)/shard_map/chrk,krhsp->kcsp/dot_general | solution.py:138
  137.0 0.8 copy.103
  137.8 8.4 %reduce-scatter.2.cloned.1.call-done = f32[256,1,2,128]{3,0,2,1:T(8,128)} async-done(((f32[256,2,2,128]{3,0,2,1:T(8,128)}), f32[256,1,2,128]{3,0,2,1:T(8,128)}) %reduce-scatter.2.cloned.1.call-update) | async-done | bytes 262160 | tf_op jit(solution)/shard_map/reduce_scatter | solution.py:139
  146.2 1.1 fusion.25
  147.3 1.0 multiply_convert_fusion.4
  148.3 2.0 %all_gather.3 = bf16[256,2,2,128]{3,0,2,1:T(8,128)(2,1)S(1)} all-gather(bf16[256,1,2,128]{3,0,2,1:T(8,128)(2,1)S(1)} %multiply_convert_fusion.4), channel_id=1, replica_groups=mesh['group'=2,'mid'=4,'freq'=2,'off'=2] {'off'}, dimensions={1}, use_global_device_ids=true | all-gather | bytes 393216 | tf_op jit(solution)/shard_map/all_gather | solution.py:141
  150.3 16.8 %fusion.12 = f32[256,2,64,2]{2,3,1,0:T(2,128)S(1)} fusion(bf16[256,1,64,2,128]{4,2,1,3,0:T(8,128)(2,1)} %get-tuple-element.8, bf16[256,1,64,2,128]{4,2,1,3,0:T(8,128)(2,1)} %get-tuple-element.7, bf16[256,2,2,128,1]{3,0,2,1,4:T(8,128)(2,1)S(1)} %bitcast.79), kind=kOutput, calls=%fused_computation.28 | convolution fusion | flops 41943040 | bytes 17301504 | tf_op jit(solution)/shard_map/kcsp,krhsp->chrk/dot_general | solution.py:142
  167.9 14.9 %all_to_all.30 = bf16[8,32,512]{2,1,0:T(8,128)(2,1)S(1)} all-to-all(bf16[8,32,512]{2,1,0:T(8,128)(2,1)S(1)} %bitcast.73), channel_id=1, replica_groups=mesh['group'=2,'mid'=4,'freq'=2,'off'=2] {'mid','freq'}, dimensions={0} | all-to-all | bytes 524288 | tf_op jit(solution)/shard_map/all_to_all | solution.py:150
  183.1 2.9 %fusion.14 = bf16[1,64,1024]{2,1,0:T(8,128)(2,1)} fusion(bf16[1024,1024]{0,1:T(8,128)(2,1)} %bitcast.71, bf16[128,1024]{1,0:T(8,128)(2,1)S(1)} %bitcast.76, s32[64]{0:T(128)S(1)} %get-tuple-element.14), kind=kOutput, calls=%fused_computation.37 | convolution fusion | flops 151216128 | bytes 2490624 | tf_op jit(solution)/shard_map/dot_general | solution.py:157
  (49 shorter events, 4.1 us)
Async XLA Ops:
  6.5 60.1 %copy-start = (bf16[1024,1024]{1,0:T(8,128)(2,1)S(1)}, bf16[1024,1024]{1,0:T(8,128)(2,1)}, u32[]{:S(2)}) copy-start(bf16[1024,1024]{1,0:T(8,128)(2,1)} %param.6) | copy-start | bytes 6291460
  6.5 60.1 %copy-start.1 = (bf16[1,64,1024]{2,1,0:T(8,128)(2,1)S(1)}, bf16[1,64,1024]{2,1,0:T(8,128)(2,1)}, u32[]{:S(2)}) copy-start(bf16[1,64,1024]{2,1,0:T(8,128)(2,1)} %param.5) | copy-start | bytes 393220
  11.3 59.2 %all-to-all-start = ((s32[8,32,1]{1,2,0:T(1,128)}), s32[8,32,1]{1,2,0:T(1,128)S(1)}, u32[]{:S(2)}, u32[]{:S(2)}) async-start(s32[8,32,1]{1,2,0:T(1,128)} %bitcast.4), calls=%async_computation | async-start | bytes 8192 | tf_op jit(solution)/shard_map/all_to_all | solution.py:118
  70.6 39.4 %all-to-all-start.1 = ((bf16[8,32,512]{2,1,0:T(8,128)(2,1)}), bf16[8,32,512]{2,1,0:T(8,128)(2,1)S(1)}, u32[]{:S(2)}, u32[]{:S(2)}) async-start(bf16[8,32,512]{2,1,0:T(8,128)(2,1)} %bitcast.8), calls=%async_computation.1 | async-start | bytes 524288 | tf_op jit(solution)/shard_map/all_to_all | solution.py:117
  76.6 69.6 %reduce-scatter.2.cloned.1.call-start = ((), (), s32[]{:S(2)}) async-start(), calls=%async_computation.4 | async-start | bytes 786432 | tf_op jit(solution)/shard_map/reduce_scatter | solution.py:139
  110.2 19.3 %collective-permute-start.1 = (bf16[1,64,2,256]{3,1,2,0:T(8,128)(2,1)S(1)}, bf16[1,64,2,256]{3,1,2,0:T(8,128)(2,1)S(1)}, u32[]{:S(2)}, u32[]{:S(2)}) collective-permute-start(bf16[1,64,2,256]{3,1,2,0:T(8,128)(2,1)S(1)} %copy.100), channel_id=1, source_target_pairs={{4,0},{8,4},{12,8},{5,1},{9,5},{13,9},{6,2},{10,6},{14,10},{7,3},{... | collective-permute-start | bytes 196616 | tf_op jit(solution)/shard_map/ppermute | solution.py:26
  111.6 18.0 %collective-permute-start = (bf16[1,64,2,256]{3,1,2,0:T(8,128)(2,1)S(1)}, bf16[1,64,2,256]{3,1,2,0:T(8,128)(2,1)S(1)}, u32[]{:S(2)}, u32[]{:S(2)}) collective-permute-start(bf16[1,64,2,256]{3,1,2,0:T(8,128)(2,1)S(1)} %copy.98), channel_id=1, source_target_pairs={{0,4},{4,8},{8,12},{1,5},{5,9},{9,13},{2,6},{6,10},{10,14},{3,7},{... | collective-permute-start | bytes 196616 | tf_op jit(solution)/shard_map/ppermute | solution.py:24
  129.8 8.1 %copy-start.2 = (f32[256]{0:T(256)S(1)}, f32[256]{0:T(256)}, u32[]{:S(2)}) copy-start(f32[256]{0:T(256)} %param.9) | copy-start | bytes 3076
Sparse Core Ops, SparseCore 0:
  137.9 8.2 reduce-scatter.1
where the time goes:
time: 193 us
  other arithmetic  99.9 us (52%)
  matrix products  30.3 us (16%)
  starting transfers between devices  19.3 us (10%)
  blocking collectives  16.9 us (9%)
  between operations  13.7 us (7%)
  waiting for transfers between devices  8.38 us (4%)
  local copies, waits for them, and re-layouts  4.32 us (2%)
    convert_element_type x1, other arithmetic, radon_table(): sine = (jnp.sin(angle) * scale_r).astype(jnp.bfloat16)  35.3 us
    neg x1, other arithmetic, radon_table(): second = jnp.stack([-sine, cosine], axis=2)  32.3 us
    dot_general x1, matrix products, on_device(): jnp.einsum('kcsp,krhsp->chrk', kept, weights, preferred_element_type=jnp....  16.8 us
    all_to_all x1, blocking collectives, on_device(): lax.all_to_all(back_rows, ('mid', 'freq'), split_axis=0, concat_axis=0, t...  14.9 us
    another operation x1, other arithmetic, radon_table(): return jnp.stack([first, second], axis=1)  13.3 us
    convert_element_type x1, other arithmetic, dft_table(): cosine = (jnp.cos(angle) * scale_f).astype(jnp.bfloat16)  9.79 us
    reduce_scatter x1, waiting for transfers between devices, on_device(): lax.psum_scatter(model_part, 'off', scatter_dimension=1, tiled=True)  8.35 us
    all_to_all x1, starting transfers between devices, on_device(): lax.all_to_all(flat_cells, ('mid', 'freq'), split_axis=0, concat_axis=0,...  7.28 us
  transfers between devices with their start and end apart: 5, of which 1 were waited for; matrix products, arithmetic and copies ran while one was open for 51% of the time, Pallas kernels for 0%

commit v1 on v0

v1 whole, which is shorter than its diff:
```python
import functools
import math

import jax
import jax.numpy as jnp
import numpy as np
from jax import lax
from jax.experimental import pallas as pl
from jax.experimental.pallas import tpu as pltpu
from jax.sharding import PartitionSpec as P

NOFF = 128
NP = 128
radon_period = 4096
VMEM = pl.BlockSpec(memory_space=pltpu.VMEM)
ANY = pl.BlockSpec(memory_space=pl.ANY)


def dft_table(n_time, n_bands, band_size):
    sample = np.arange(n_time, dtype=np.int64)[:, None]
    freq_index = np.arange(n_bands * band_size, dtype=np.int64)[None, :]
    angle = 2.0 * np.pi * (sample * freq_index % n_time) / n_time
    scale_f = 1.0 / math.sqrt(n_time)
    cosine = (np.cos(angle) * scale_f).reshape(n_time, n_bands, band_size)
    sine = (-np.sin(angle) * scale_f).reshape(n_time, n_bands, band_size)
    table = np.stack([cosine, sine], axis=2).reshape(n_time, n_bands * 2 * band_size)
    return table.astype(np.float32).astype(jnp.bfloat16)


def radon_table(n_freqs, n_off):
    freq_index = np.arange(n_freqs, dtype=np.int64)[:, None, None]
    offset_index = np.arange(NOFF, dtype=np.int64)[None, :, None]
    slowness = np.arange(NP, dtype=np.int64)[None, None, :]
    turns = freq_index * slowness % radon_period * (offset_index * offset_index % radon_period) % radon_period
    circle = 2.0 * np.pi * np.arange(radon_period) / radon_period
    scale_r = 1.0 / math.sqrt(NOFF)
    cosine = (np.cos(circle) * scale_r).astype(np.float32).astype(jnp.bfloat16)[turns]
    sine = (np.sin(circle) * scale_r).astype(np.float32).astype(jnp.bfloat16)[turns]
    both = np.stack([cosine, sine], axis=1).reshape(n_freqs, 2, n_off, NOFF // n_off, NP)
    return np.ascontiguousarray(both.transpose(2, 0, 1, 3, 4)).reshape(n_off, n_freqs, 2 * NOFF // n_off, NP)


def signal(barrier, **device):
    pl.semaphore_signal(barrier, inc=1, device_id=device, device_id_type=pl.DeviceIdType.MESH)


def send(src, dst, send_sem, recv_sem, **device):
    return pltpu.make_async_remote_copy(
        src_ref=src,
        dst_ref=dst,
        send_sem=send_sem,
        recv_sem=recv_sem,
        device_id=device,
        device_id_type=pl.DeviceIdType.MESH,
    )


def spread_kernel(n_mid, n_freq, blocks, rows, own_sem, x_send, x_recv, z_send, z_recv):
    mid = lax.axis_index("mid")
    freq = lax.axis_index("freq")
    has = (mid < n_mid - 1, mid > 0)
    barrier = pltpu.get_barrier_semaphore()
    for d in range(1, n_freq):
        signal(barrier, freq=(freq + d) % n_freq)
    for way, step in ((0, 1), (1, -1)):

        @pl.when(has[way])
        def _():
            signal(barrier, mid=mid + step)

    pl.semaphore_wait(barrier, n_freq - 1 + has[0].astype(jnp.int32) + has[1].astype(jnp.int32))
    own = pltpu.make_async_copy(blocks.at[freq], rows.at[mid, freq], own_sem)
    own.start()
    across = []
    for d in range(1, n_freq):
        other = (freq + d) % n_freq
        across.append(send(blocks.at[other], rows.at[mid, freq], x_send.at[d], x_recv.at[d], freq=other))
        across[-1].start()

    def hop(way, step, s, d):
        start = mid - step * s
        origin = (freq + n_freq - d) % n_freq
        src = blocks.at[freq] if s == 0 and d == 0 else rows.at[start, origin]
        return send(src, rows.at[start, origin], z_send.at[way, s, d], z_recv.at[way, s, d], mid=mid + step)

    for s in range(n_mid):
        for d in range(n_freq):
            if s == 0 and d > 0:
                across[d - 1].wait_recv()
            for way, step in ((0, 1), (1, -1)):
                behind = mid - step * s
                real = (behind >= 0) & (behind < n_mid)
                if s > 0:

                    @pl.when(real)
                    def _():
                        hop(way, step, s - 1, d).wait_recv()

                if s < n_mid - 1:

                    @pl.when(real & has[way])
                    def _():
                        hop(way, step, s, d).start()

    own.wait()
    for copy in across:
        copy.wait_send()
    for s in range(n_mid - 1):
        for d in range(n_freq):
            for way, step in ((0, 1), (1, -1)):
                behind = mid - step * s

                @pl.when((behind >= 0) & (behind < n_mid) & has[way])
                def _():
                    hop(way, step, s, d).wait_send()


def spread(blocks, n_mid):
    n_freq = blocks.shape[0]
    return pl.pallas_call(
        functools.partial(spread_kernel, n_mid, n_freq),
        out_shape=jax.ShapeDtypeStruct((n_mid,) + blocks.shape, blocks.dtype),
        in_specs=[VMEM],
        out_specs=VMEM,
        scratch_shapes=[
            pltpu.SemaphoreType.DMA,
            pltpu.SemaphoreType.DMA((n_freq,)),
            pltpu.SemaphoreType.DMA((n_freq,)),
            pltpu.SemaphoreType.DMA((2, n_mid, n_freq)),
            pltpu.SemaphoreType.DMA((2, n_mid, n_freq)),
        ],
        compiler_params=pltpu.CompilerParams(collective_id=0, has_side_effects=True),
    )(blocks)


def return_kernel(n_mid, n_freq, blocks, got, own_sem, send_sem, recv_sem):
    mid = lax.axis_index("mid")
    freq = lax.axis_index("freq")
    others = [(a, b) for a in range(n_mid) for b in range(n_freq) if (a, b) != (0, 0)]
    barrier = pltpu.get_barrier_semaphore()
    for a, b in others:
        signal(barrier, mid=(mid + a) % n_mid, freq=(freq + b) % n_freq)
    pl.semaphore_wait(barrier, len(others))
    copies = []
    for a, b in others:
        to_mid, to_freq = (mid + a) % n_mid, (freq + b) % n_freq
        copies.append(
            send(
                blocks.at[to_mid, to_freq],
                got.at[mid, freq],
                send_sem.at[a, b],
                recv_sem.at[a, b],
                mid=to_mid,
                freq=to_freq,
            )
        )
        copies[-1].start()
    own = pltpu.make_async_copy(blocks.at[mid, freq], got.at[mid, freq], own_sem)
    own.start()
    own.wait()
    for copy in copies:
        copy.wait()


def give_back(blocks):
    n_mid, n_freq = blocks.shape[:2]
    return pl.pallas_call(
        functools.partial(return_kernel, n_mid, n_freq),
        out_shape=jax.ShapeDtypeStruct(blocks.shape, blocks.dtype),
        in_specs=[VMEM],
        out_specs=VMEM,
        scratch_shapes=[
            pltpu.SemaphoreType.DMA,
            pltpu.SemaphoreType.DMA((n_mid, n_freq)),
            pltpu.SemaphoreType.DMA((n_mid, n_freq)),
        ],
        compiler_params=pltpu.CompilerParams(collective_id=1, has_side_effects=True),
    )(blocks)


def radon_kernel(n_off, chunk, x, level, table, out, weights, part, got, t_sem, send_sem, recv_sem):
    freq = lax.axis_index("freq")
    off = lax.axis_index("off")
    band, rows, width = x.shape
    half = rows // 2
    n_chunks = band // chunk

    def span(j):
        return pl.ds(pl.multiple_of(j * chunk, chunk), chunk)

    def fetch(j):
        first = pl.multiple_of(freq * band + j * chunk, chunk)
        return pltpu.make_async_copy(table.at[off, pl.ds(first, chunk)], weights.at[span(j)], t_sem.at[j])

    def pass_on(j, d):
        return send(
            part.at[span(j)],
            got.at[d - 1, span(j)],
            send_sem.at[d - 1, j],
            recv_sem.at[d - 1, j],
            off=(off + d) % n_off,
        )

    @pl.loop(0, n_chunks)
    def _(j):
        fetch(j).start()

    barrier = pltpu.get_barrier_semaphore()
    for d in range(1, n_off):
        signal(barrier, off=(off + d) % n_off)
    pl.semaphore_wait(barrier, n_off - 1)

    @pl.loop(0, n_chunks)
    def _(j):
        fetch(j).wait()
        part[span(j)] = lax.dot_general(
            x[span(j)], weights[span(j)], (((2,), (1,)), ((0,), (0,))), preferred_element_type=jnp.float32
        )
        for d in range(1, n_off):
            pass_on(j, d).start()

    keep = (lax.broadcasted_iota(jnp.int32, (chunk, rows, NP), 2) >= NP // 4).astype(jnp.float32)

    @pl.loop(0, n_chunks)
    def _(j):
        model = part[span(j)]
        for d in range(1, n_off):
            pass_on(j, d).wait_recv()
            model = model + got[d - 1, span(j)]
        squares = model * model
        power = squares + pltpu.roll(squares, half, 1)
        lev = level[span(j)]
        factor = power / (power + lev * lev) * keep
        kept = (model * factor).astype(jnp.bfloat16)
        both = lax.dot_general(
            kept, weights[span(j)], (((2,), (2,)), ((0,), (0,))), preferred_element_type=jnp.float32
        )
        out[span(j)] = both + pltpu.roll(pltpu.roll(both, half, 1), width // 2, 2)

    @pl.loop(0, n_chunks)
    def _(j):
        for d in range(1, n_off):
            pass_on(j, d).wait_send()


def radon(x, level, table, n_off):
    band, rows, width = x.shape
    chunk = min(32, band)
    n_chunks = band // chunk
    return pl.pallas_call(
        functools.partial(radon_kernel, n_off, chunk),
        out_shape=jax.ShapeDtypeStruct(x.shape, jnp.float32),
        in_specs=[VMEM, VMEM, ANY],
        out_specs=VMEM,
        scratch_shapes=[
            pltpu.VMEM((band, width, NP), jnp.bfloat16),
            pltpu.VMEM((band, rows, NP), jnp.float32),
            pltpu.VMEM((n_off - 1, band, rows, NP), jnp.float32),
            pltpu.SemaphoreType.DMA((n_chunks,)),
            pltpu.SemaphoreType.DMA((n_off - 1, n_chunks)),
            pltpu.SemaphoreType.DMA((n_off - 1, n_chunks)),
        ],
        compiler_params=pltpu.CompilerParams(
            collective_id=2, has_side_effects=True, vmem_limit_bytes=32 * 1024 * 1024
        ),
    )(x, level, table)


def on_device(dft, weights, traces, time_filter, midpoint_of, offset_of, shrink_level):
    n_mid = lax.axis_size("mid")
    n_freq = lax.axis_size("freq")
    n_off = lax.axis_size("off")
    me_mid = lax.axis_index("mid")
    me_freq = lax.axis_index("freq")
    me_off = lax.axis_index("off")
    tr_dev = traces.shape[1]
    band = shrink_level.shape[0]
    noff_dev = NOFF // n_off
    cmp_dev = n_freq * tr_dev // noff_dev
    capacity = 2 * tr_dev // n_mid
    n_send = n_mid * n_freq
    n_cells = cmp_dev * noff_dev
    width = 2 * band
    f32, bf16 = jnp.float32, jnp.bfloat16

    filtered = jnp.dot(traces[0], time_filter, preferred_element_type=f32).astype(bf16)
    spectra = jnp.dot(filtered, dft, preferred_element_type=f32).astype(bf16)
    blocks = jnp.transpose(spectra.reshape(tr_dev, n_freq, width), (1, 0, 2))
    rows = spread(blocks, n_mid).reshape(n_send * tr_dev, width)

    mids = midpoint_of[0]
    offs = offset_of[0] % noff_dev
    cell = jnp.arange(n_cells, dtype=jnp.int32)[:, None]
    apart = jnp.abs(mids[None, :] - (me_mid * cmp_dev + cell // noff_dev))
    hit = offs[None, :] == cell % noff_dev
    mix = jnp.where(hit & (apart < 2), jnp.where(apart == 0, 0.5, 0.25), 0.0).astype(bf16)
    smooth = jnp.dot(mix, rows, preferred_element_type=f32).astype(bf16)
    smooth = jnp.transpose(smooth.reshape(cmp_dev, noff_dev, 2, band), (3, 2, 0, 1))
    re, im = smooth[:, 0], smooth[:, 1]
    first = jnp.concatenate([re, -im], axis=2)
    second = jnp.concatenate([im, re], axis=2)
    x = jnp.concatenate([first, second, second, -first], axis=1)
    level = jnp.broadcast_to(shrink_level[:, None, None], (band, 1, NP))
    mult = radon(x, level, weights, n_off)
    mult = mult[:, : 2 * cmp_dev, :noff_dev].astype(bf16).reshape(band, 2, cmp_dev, noff_dev)
    mult = jnp.transpose(mult, (2, 3, 1, 0)).reshape(n_cells, width)

    owner = (mids // cmp_dev).reshape(n_send, tr_dev)
    trace_cell = (mids % cmp_dev * noff_dev + offs).reshape(n_send, tr_dev)
    place = jnp.arange(tr_dev, dtype=jnp.int32)
    before = (owner[:, :, None] == owner[:, None, :]) & (place[None, None, :] < place[None, :, None])
    rank = jnp.sum(before.astype(jnp.int32), axis=2)
    slots = jnp.arange(capacity, dtype=jnp.int32)
    mine = (owner == me_mid)[:, None, :] & (rank[:, None, :] == slots[None, :, None])
    slot_cell = jnp.sum(jnp.where(mine, trace_cell[:, None, :] + 1, 0), axis=2) - 1
    pick = (slot_cell.reshape(-1)[:, None] == jnp.arange(n_cells, dtype=jnp.int32)[None, :]).astype(bf16)
    back = jnp.dot(pick, mult, preferred_element_type=f32).astype(bf16)
    returned = give_back(back.reshape(n_mid, n_freq, capacity, width))

    me = me_mid * n_freq + me_freq
    own_slot = owner[me] * capacity + rank[me]
    take = (own_slot[:, None] == jnp.arange(n_mid * capacity, dtype=jnp.int32)[None, :]).astype(bf16)
    ordered = jnp.transpose(returned, (0, 2, 1, 3)).reshape(n_mid * capacity, n_freq * width)
    own_mult = jnp.dot(take, ordered, preferred_element_type=f32)
    clean = (spectra.astype(f32) - own_mult).astype(bf16)
    total = lax.dot_general(clean, dft, (((1,), (1,)), ((), ())), preferred_element_type=f32)
    return (2.0 * total).astype(bf16)[None]


def solution(mesh):
    n_freq = mesh.shape["freq"]

    def run(traces, time_filter, midpoint_of, offset_of, shrink_level):
        n_freqs = shrink_level.shape[0]
        dft = dft_table(traces.shape[2], n_freq, n_freqs // n_freq)
        weights = radon_table(n_freqs, mesh.shape["off"])
        return jax.shard_map(
            on_device,
            mesh=mesh,
            in_specs=(
                P(),
                P(),
                P("off", ("group", "mid", "freq"), None),
                P(),
                P("off", "group"),
                P("off", "group"),
                P("freq"),
            ),
            out_specs=P("off", ("group", "mid", "freq"), None),
            check_vma=False,
        )(jnp.asarray(dft), jnp.asarray(weights), traces, time_filter, midpoint_of, offset_of, shrink_level)

    return run
```

time: 193 us -> 58 us (0.30)
  other arithmetic: 99.9 us -> 5.21 us
  Pallas kernels: 0 us -> 40.7 us
  matrix products: 30.3 us -> 7.98 us
  starting transfers between devices: 19.3 us -> 0 us
  blocking collectives: 16.9 us -> 0 us
  between operations: 13.7 us -> 0.17 us
  waiting for transfers between devices: 8.38 us -> 0 us
    convert_element_type x7 -> x0, other arithmetic: 46.2 us -> none  [the longest x1 35.3 us: radon_table(): sine = (jnp.sin(angle) * scale_r).astype(jnp.bfloat16)]
    pallas_call x0 -> x3, Pallas kernels: none -> 40.7 us  [the longest x1 19.7 us: spread(): pl.pallas_call(functools.partial(spread_kernel, n_mid, n_freq), out_shape...]
    neg x1 -> x2, other arithmetic: 32.3 us -> 0.51 us  [the longest x1 0.39 us: on_device(): x = jnp.concatenate([first, second, second, -first], axis=1)]
    dot_general x7 -> x4, matrix products: 30.3 us -> 7.98 us  [the longest x1 3.14 us: on_device(): lax.dot_general(clean, dft, (((1,), (1,)), ((), ())), preferred_element_t...]
    another operation x3 -> x0, other arithmetic: 16.2 us -> none  [the longest x1 13.3 us: radon_table(): return jnp.stack([first, second], axis=1)]
    all_to_all x1 -> x0, blocking collectives: 14.9 us -> none  [on_device(): lax.all_to_all(back_rows, ('mid', 'freq'), split_axis=0, concat_axis=0, t...]
    all_to_all x2 -> x0, starting transfers between devices: 13.3 us -> none  [the longest x1 7.28 us: on_device(): lax.all_to_all(flat_cells, ('mid', 'freq'), split_axis=0, concat_axis=0,...]
    reduce_scatter x1 -> x0, waiting for transfers between devices: 8.35 us -> none  [on_device(): lax.psum_scatter(model_part, 'off', scatter_dimension=1, tiled=True)]
  transfers between devices with their start and end apart: 5 -> 0, of which waited for: 1 -> 0; matrix products, arithmetic and copies ran while one was open for 51% -> 0% of each run, Pallas kernels for 0% -> 0%
where the time goes in v1:
time: 58 us; the launch traced here: 57.7 us
  Pallas kernels  40.7 us (70%)
  matrix products  7.98 us (14%)
  other arithmetic  5.21 us (9%)
  local copies, waits for them, and re-layouts  3.65 us (6%)
    pallas_call x1, Pallas kernels, spread(): pl.pallas_call(functools.partial(spread_kernel, n_mid, n_freq), out_shape...  19.7 us
    pallas_call x1, Pallas kernels, radon(): pl.pallas_call(functools.partial(radon_kernel, n_off, chunk), out_shape=j...  10.5 us
    pallas_call x1, Pallas kernels, give_back(): pl.pallas_call(functools.partial(return_kernel, n_mid, n_freq), out_shape...  10.5 us
    dot_general x1, matrix products, on_device(): lax.dot_general(clean, dft, (((1,), (1,)), ((), ())), preferred_element_t...  3.14 us
    unnamed x2, other arithmetic  2.81 us
    dot_general x1, matrix products, on_device(): spectra = jnp.dot(filtered, dft, preferred_element_type=f32).astype(bf16)  2.55 us
    dot_general x1, matrix products, on_device(): smooth = jnp.dot(mix, rows, preferred_element_type=f32).astype(bf16)  1.33 us
    concatenate x1, other arithmetic, on_device(): x = jnp.concatenate([first, second, second, -first], axis=1)  1.3 us

profile of v1, /device:TPU:0, one launch (start us, length us, event | category | flops | bytes accessed | tf_op | source)
XLA Modules:
  0.0 57.7 jit_solution(16074066366415986623)
XLA Ops:
  0.0 0.5 broadcast.272
  0.5 1.5 %reduce.7 = s32[512]{0:T(512)S(1)} reduce(s32[1,512]{1,0:T(1,128)} %param.9, s32[]{:T(128)} %broadcast.272), dimensions={0}, to_apply=%param.9.reduce_sub_computation.3 | reduce | bytes 4100 | tf_op args[2]
  2.0 0.1 squeeze.18
  2.1 1.3 %fusion.36 = (s32[512]{0:T(512)S(1)}, s32[1,512]{1,0:T(1,128)S(1)}) fusion(s32[1,512]{1,0:T(1,128)} %param.10, s32[]{:T(128)} %broadcast.272), kind=kLoop, calls=%fused_computation.74 | loop fusion | flops 5632 | bytes 6148 | tf_op args[3]
  3.4 0.1 squeeze.19
  3.5 0.3 convert_reduce_fusion
  3.9 0.2 select_reduce_fusion
  4.1 0.1 sub.38
  4.2 2.5 %convolution_convert_fusion.2 = bf16[64,1024]{1,0:T(8,128)(2,1)S(1)} fusion(bf16[1024,1024]{1,0:T(8,128)(2,1)} %constant.93.clone, bf16[1024,1024]{1,0:T(8,128)(2,1)S(1)} %copy-done, bf16[1,64,1024]{2,1,0:T(8,128)(2,1)} %param.7), kind=kOutput, calls=%fused_computation.6 | convolution fusion | flops 268566528 | bytes 4456448 | tf_op jit(solution)/shard_map/dot_general | solution.py:287
  6.7 0.7 %copy.21 = bf16[8,2,8,512]{3,2,0,1:T(8,128)(2,1)} copy(bf16[8,2,8,512]{3,2,1,0:T(8,128)(2,1)S(1)} %bitcast.43) | data formatting | bytes 262144 | tf_op jit(solution)/shard_map/reshape | solution.py:288
  7.4 0.3 broadcast_in_dim.48.level
  7.7 19.7 %shard_map.73 = bf16[4,2,64,512]{3,2,1,0:T(8,128)(2,1)} custom-call(bf16[2,64,512]{2,1,0:T(8,128)(2,1)} %bitcast.51), custom_call_target="tpu_custom_call" | custom-call | tf_op jit(solution)/shard_map/pallas_call | solution.py:120
  27.5 1.3 %convolution_convert_fusion.1 = bf16[128,512]{1,0:T(8,128)(2,1)S(1)} fusion(bf16[512,512]{1,0:T(8,128)(2,1)} %bitcast.49, s32[128]{0:T(128)S(1)} %get-tuple-element.12, s32[512]{0:T(512)S(1)} %bitcast.53, s32[512]{0:T(512)S(1)} %bitcast.54, s32[128]{0:T(128)S(1)} %get-tuple-element.11), kind=kOutput, calls=%fused_computation.5 | convolution fusion | flops 67764224 | bytes 660480 | tf_op jit(solution)/shard_map/dot_general | solution.py:297
  28.9 0.2 copy.14
  29.1 0.1 fusion.35
  29.2 0.2 slice_bitcast_fusion
  29.4 0.4 maximum_negate_fusion
  29.8 1.3 %pad_maximum_fusion.x = bf16[256,8,128]{2,1,0:T(8,128)(2,1)S(1)} fusion(bf16[256,2,128]{2,1,0:T(2,128)(2,1)S(1)} %maximum_negate_fusion, bf16[256,2,64]{2,1,0:T(2,128)(2,1)S(1)} %get-tuple-element.8, bf16[256,2,64]{2,1,0:T(2,128)(2,1)S(1)} %get-tuple-element.7, bf16[256,2,64]{2,1,0:T(2,128)(2,1)S(1)} %fusion.35), kind=kLoop, calls=%fused_computation.10 | loop fusion | flops 3670016 | bytes 851968 | tf_op jit(solution)/shard_map/concatenate | solution.py:302
  31.1 10.5 %shard_map.74 = f32[256,8,128]{2,1,0:T(8,128)S(1)} custom-call(bf16[256,8,128]{2,1,0:T(8,128)(2,1)S(1)} %pad_maximum_fusion.x, f32[256,1,128]{2,1,0:T(1,128)S(1)} %broadcast_in_dim.48.level, bf16[2,512,128,128]{3,2,1,0:T(8,128)(2,1)} %constant.94.clone.table), custom_call_target="tpu_custom_call" | custom-call | tf_op jit(solution)/shard_map/pallas_call | solution.py:250
  41.6 0.2 copy.15
  41.8 1.0 %convolution_convert_fusion = bf16[256,512]{1,0:T(8,128)(2,1)} fusion(bf16[128,512]{1,0:T(8,128)(2,1)S(1)} %bitcast.50, s32[256]{0:T(256)S(1)} %sub.38), kind=kOutput, calls=%fused_computation | convolution fusion | flops 33718272 | bytes 394240 | tf_op jit(solution)/shard_map/dot_general | solution.py:317
  42.8 10.5 %shard_map.75 = bf16[4,2,32,512]{3,2,1,0:T(8,128)(2,1)} custom-call(bf16[4,2,32,512]{3,2,1,0:T(8,128)(2,1)} %bitcast.44), custom_call_target="tpu_custom_call" | custom-call | tf_op jit(solution)/shard_map/pallas_call | solution.py:167
  53.3 1.2 %copy.16 = bf16[4,32,2,512]{3,2,1,0:T(2,128)(2,1)S(1)} copy(bf16[4,32,2,512]{3,1,2,0:T(8,128)(2,1)} %bitcast.46) | data formatting | bytes 524288 | tf_op jit(solution)/shard_map/transpose | solution.py:323
  54.5 3.1 %fusion.2 = bf16[1,64,1024]{2,1,0:T(8,128)(2,1)} fusion(bf16[1024,1024]{1,0:T(8,128)(2,1)} %constant.93.clone, bf16[128,1024]{1,0:T(8,128)(2,1)S(1)} %bitcast.48, bf16[64,1024]{1,0:T(8,128)(2,1)S(1)} %convolution_convert_fusion.2, s32[64]{0:T(128)S(1)} %add_bitcast_fusion), kind=kOutput, calls=%fused_computation.8 | convolution fusion | flops 151330816 | bytes 2621696 | tf_op jit(solution)/shard_map/dot_general | solution.py:326
  (16 shorter events, 0.2 us)
Async XLA Ops:
  0.0 4.2 %copy-start = (bf16[1024,1024]{1,0:T(8,128)(2,1)S(1)}, bf16[1024,1024]{1,0:T(8,128)(2,1)}, u32[]{:S(2)}) copy-start(bf16[1024,1024]{1,0:T(8,128)(2,1)} %param.8) | copy-start | bytes 6291460
  4.2 3.2 %copy-start.2 = (f32[256]{0:T(256)S(1)}, f32[256]{0:T(256)}, u32[]{:S(2)}) copy-start(f32[256]{0:T(256)} %param.11) | copy-start | bytes 3076
  4.2 23.3 %copy-start.1 = (s32[1,512]{1,0:T(1,128)S(1)}, s32[1,512]{1,0:T(1,128)}, u32[]{:S(2)}) copy-start(s32[1,512]{1,0:T(1,128)} %param.9) | copy-start | bytes 6148

commit v2 on v0

v2 whole, which is shorter than its diff:
```python
import functools
import math

import jax
import jax.numpy as jnp
import numpy as np
from jax import lax
from jax.experimental import pallas as pl
from jax.experimental.pallas import tpu as pltpu
from jax.sharding import PartitionSpec as P

NOFF = 128
NP = 128
radon_period = 4096
VMEM = pl.BlockSpec(memory_space=pltpu.VMEM)
ANY = pl.BlockSpec(memory_space=pl.ANY)


def dft_table(n_time, n_bands, band_size):
    sample = np.arange(n_time, dtype=np.int64)[:, None]
    freq_index = np.arange(n_bands * band_size, dtype=np.int64)[None, :]
    angle = 2.0 * np.pi * (sample * freq_index % n_time) / n_time
    scale_f = 1.0 / math.sqrt(n_time)
    cosine = (np.cos(angle) * scale_f).reshape(n_time, n_bands, band_size)
    sine = (-np.sin(angle) * scale_f).reshape(n_time, n_bands, band_size)
    table = np.stack([cosine, sine], axis=2).reshape(n_time, n_bands * 2 * band_size)
    return table.astype(np.float32).astype(jnp.bfloat16)


def radon_table(n_freqs):
    freq_index = np.arange(n_freqs, dtype=np.int64)[:, None, None]
    offset_index = np.arange(NOFF, dtype=np.int64)[None, :, None]
    slowness = np.arange(NP, dtype=np.int64)[None, None, :]
    turns = freq_index * slowness % radon_period * (offset_index * offset_index % radon_period) % radon_period
    circle = 2.0 * np.pi * np.arange(radon_period) / radon_period
    scale_r = 1.0 / math.sqrt(NOFF)
    cosine = (np.cos(circle) * scale_r).astype(np.float32).astype(jnp.bfloat16)[turns]
    sine = (np.sin(circle) * scale_r).astype(np.float32).astype(jnp.bfloat16)[turns]
    return np.stack([cosine, sine], axis=1).reshape(n_freqs, 2 * NOFF, NP)


def signal(barrier, **device):
    pl.semaphore_signal(barrier, inc=1, device_id=device, device_id_type=pl.DeviceIdType.MESH)


def send(src, dst, send_sem, recv_sem, **device):
    return pltpu.make_async_remote_copy(
        src_ref=src,
        dst_ref=dst,
        send_sem=send_sem,
        recv_sem=recv_sem,
        device_id=device,
        device_id_type=pl.DeviceIdType.MESH,
    )


def place(sizes):
    names = ("off", "mid", "freq")
    here = [lax.axis_index(name) for name in names]
    index = (here[0] * sizes[1] + here[1]) * sizes[2] + here[2]
    total = sizes[0] * sizes[1] * sizes[2]

    def ahead(i):
        there = (index + i) % total
        return there, dict(off=there // (sizes[1] * sizes[2]), mid=there // sizes[2] % sizes[1], freq=there % sizes[2])

    return index, total, ahead


def swap_kernel(sizes, with_ids, *refs):
    if with_ids:
        blocks, ids, got, got_ids, own_sem, send_sem, recv_sem, id_own, id_send, id_recv = refs
    else:
        blocks, got, own_sem, send_sem, recv_sem = refs
    index, total, ahead = place(sizes)
    n_off = sizes[0]
    barrier = pltpu.get_barrier_semaphore()

    @pl.loop(1, total)
    def _(i):
        signal(barrier, **ahead(i)[1])

    own = pltpu.make_async_copy(blocks.at[index], got.at[index], own_sem)
    own.start()
    pl.semaphore_wait(barrier, total - 1)

    def block_copy(i):
        there, device = ahead(i)
        return send(blocks.at[there], got.at[index], send_sem.at[i], recv_sem.at[i], **device)

    def id_copy(d):
        off = lax.axis_index("off")
        return send(ids, got_ids.at[off], id_send.at[d], id_recv.at[d], off=(off + d) % n_off)

    if with_ids:
        own_ids = pltpu.make_async_copy(ids, got_ids.at[lax.axis_index("off")], id_own)
        own_ids.start()
        for d in range(1, n_off):
            id_copy(d).start()

    @pl.loop(1, total)
    def _(i):
        block_copy(i).start()

    own.wait()
    if with_ids:
        own_ids.wait()
        for d in range(1, n_off):
            id_copy(d).wait()

    @pl.loop(1, total)
    def _(i):
        block_copy(i).wait()


def swap(blocks, sizes, collective_id, ids=None):
    total, n_off = blocks.shape[0], sizes[0]
    dma = pltpu.SemaphoreType.DMA
    shapes = [jax.ShapeDtypeStruct(blocks.shape, blocks.dtype)]
    scratch = [dma, dma((total,)), dma((total,))]
    operands = [blocks]
    if ids is not None:
        shapes.append(jax.ShapeDtypeStruct((n_off,) + ids.shape, ids.dtype))
        scratch += [dma, dma((n_off,)), dma((n_off,))]
        operands.append(ids)
    return pl.pallas_call(
        functools.partial(swap_kernel, sizes, ids is not None),
        out_shape=shapes,
        in_specs=[VMEM] * len(operands),
        out_specs=[VMEM] * len(shapes),
        scratch_shapes=scratch,
        compiler_params=pltpu.CompilerParams(collective_id=collective_id, has_side_effects=True),
    )(*operands)


def radon_kernel(n_mid, n_off, smooth, level, table, out, weights, sem):
    count, mids = smooth.shape[1:3]
    q = (lax.axis_index("freq") * n_mid + lax.axis_index("mid")) * n_off + lax.axis_index("off")
    fetch = pltpu.make_async_copy(table.at[pl.ds(q * count, count)], weights, sem)
    fetch.start()
    re = smooth[0].astype(jnp.float32)
    im = smooth[1].astype(jnp.float32)
    first = jnp.concatenate([re, -im], axis=2)
    second = jnp.concatenate([im, re], axis=2)
    x = jnp.concatenate([first, second], axis=1).astype(jnp.bfloat16)
    fetch.wait()
    model = lax.dot_general(x, weights[...], (((2,), (1,)), ((0,), (0,))), preferred_element_type=jnp.float32)
    model_re, model_im = model[:, :mids], model[:, mids:]
    power = model_re * model_re + model_im * model_im
    keep = (lax.broadcasted_iota(jnp.int32, power.shape, 2) >= NP // 4).astype(jnp.float32)
    lev = level[...]
    factor = power / (power + lev * lev) * keep
    kept = jnp.concatenate([model_re * factor, model_im * factor], axis=1).astype(jnp.bfloat16)
    both = lax.dot_general(kept, weights[...], (((2,), (2,)), ((0,), (0,))), preferred_element_type=jnp.float32)
    out[0] = (both[:, :mids, :NOFF] + both[:, mids:, NOFF:]).astype(jnp.bfloat16)
    out[1] = (both[:, mids:, :NOFF] - both[:, :mids, NOFF:]).astype(jnp.bfloat16)


def radon(smooth, level, table, n_mid, n_off):
    count = smooth.shape[1]
    return pl.pallas_call(
        functools.partial(radon_kernel, n_mid, n_off),
        out_shape=jax.ShapeDtypeStruct(smooth.shape, jnp.bfloat16),
        in_specs=[VMEM, VMEM, ANY],
        out_specs=VMEM,
        scratch_shapes=[pltpu.VMEM((count, 2 * NOFF, NP), jnp.bfloat16), pltpu.SemaphoreType.DMA],
        compiler_params=pltpu.CompilerParams(vmem_limit_bytes=24 * 1024 * 1024),
    )(smooth, level, table)


def on_device(dft, weights, traces, time_filter, midpoint_of, offset_of, shrink_level):
    n_mid = lax.axis_size("mid")
    n_freq = lax.axis_size("freq")
    n_off = lax.axis_size("off")
    sizes = (n_off, n_mid, n_freq)
    total = n_off * n_mid * n_freq
    me_mid = lax.axis_index("mid")
    me_off = lax.axis_index("off")
    tr_dev = traces.shape[1]
    count = shrink_level.shape[0] // (n_mid * n_off)
    width = 2 * count
    pack = max(1, min(tr_dev, 128 // width))
    n_traces = total * tr_dev
    n_mids = n_traces // NOFF
    f32, bf16 = jnp.float32, jnp.bfloat16

    filtered = jnp.dot(traces[0], time_filter, preferred_element_type=f32).astype(bf16)
    spectra = jnp.dot(filtered, dft, preferred_element_type=f32).astype(bf16)
    blocks = spectra.reshape(pack, tr_dev // pack, total, width)
    blocks = jnp.transpose(blocks, (2, 1, 0, 3)).reshape(total, tr_dev // pack, pack * width)
    rows, ids = swap(blocks, sizes, 0, midpoint_of * NOFF + offset_of)
    rows = rows.reshape(total, tr_dev // pack, pack, width)
    rows = jnp.transpose(rows, (0, 2, 1, 3)).reshape(n_traces, width)
    cell_of = ids.reshape(n_traces)

    small = n_traces <= 4096
    if small:
        cells = jnp.arange(n_traces, dtype=jnp.int32)[None, :]
        away = jnp.abs(cell_of[:, None] - cells)
        mix = jnp.where(away == 0, 0.5, jnp.where(away == NOFF, 0.25, 0.0)).astype(bf16)
        smooth = lax.dot_general(rows, mix, (((0,), (0,)), ((), ())), preferred_element_type=f32)
        smooth = smooth.astype(bf16).reshape(2, count, n_mids, NOFF)
    else:
        gather = jnp.zeros((n_traces, width), bf16).at[cell_of].set(rows)
        edged = jnp.pad(gather.reshape(n_mids, NOFF, 2, count).astype(f32), ((1, 1), (0, 0), (0, 0), (0, 0)))
        smooth = ((edged[:-2] + 2.0 * edged[1:-1] + edged[2:]) * 0.25).astype(bf16)
        smooth = jnp.transpose(smooth, (2, 3, 0, 1))
    own_levels = lax.dynamic_slice_in_dim(shrink_level, (me_mid * n_off + me_off) * count, count)
    level = jnp.broadcast_to(own_levels[:, None, None], (count, 1, NP))
    mult = radon(smooth, level, weights, n_mid, n_off).reshape(width, n_traces)
    if small:
        pick = (cell_of[:, None] == cells).astype(bf16)
        back = lax.dot_general(pick, mult, (((1,), (1,)), ((), ())), preferred_element_type=f32).astype(bf16)
    else:
        back = jnp.transpose(mult)[cell_of]
    back = back.reshape(total, pack, tr_dev // pack, width)
    back = jnp.transpose(back, (0, 2, 1, 3)).reshape(total, tr_dev // pack, pack * width)
    (returned,) = swap(back, sizes, 1)
    returned = returned.reshape(total, tr_dev // pack, pack, width)
    own_mult = jnp.transpose(returned, (2, 1, 0, 3)).reshape(tr_dev, total * width)
    clean = (spectra.astype(f32) - own_mult.astype(f32)).astype(bf16)
    sums = lax.dot_general(clean, dft, (((1,), (1,)), ((), ())), preferred_element_type=f32)
    return (2.0 * sums).astype(bf16)[None]


def solution(mesh):
    n_freq, n_mid, n_off = (mesh.shape[name] for name in ("freq", "mid", "off"))

    def run(traces, time_filter, midpoint_of, offset_of, shrink_level):
        n_freqs = shrink_level.shape[0]
        n_time = traces.shape[2]
        pieces = n_freq * n_mid * n_off
        dft = dft_table(n_time, pieces, n_freqs // pieces).reshape(n_time, n_freq, n_mid, n_off, -1)
        dft = np.ascontiguousarray(dft.transpose(0, 3, 2, 1, 4)).reshape(n_time, 2 * n_freqs)
        weights = radon_table(n_freqs)
        return jax.shard_map(
            on_device,
            mesh=mesh,
            in_specs=(
                P(),
                P(),
                P("off", ("group", "mid", "freq"), None),
                P(),
                P("off", "group"),
                P("off", "group"),
                P("freq"),
            ),
            out_specs=P("off", ("group", "mid", "freq"), None),
            check_vma=False,
        )(jnp.asarray(dft), jnp.asarray(weights), traces, time_filter, midpoint_of, offset_of, shrink_level)

    return run
```

time: 193 us -> 40.5 us (0.21)
  other arithmetic: 99.9 us -> 1.28 us
  Pallas kernels: 0 us -> 23.9 us
  matrix products: 30.3 us -> 8.65 us
  starting transfers between devices: 19.3 us -> 0 us
  blocking collectives: 16.9 us -> 0 us
  between operations: 13.7 us -> 0.14 us
  waiting for transfers between devices: 8.38 us -> 0 us
  local copies, waits for them, and re-layouts: 4.32 us -> 6.28 us
    convert_element_type x7 -> x0, other arithmetic: 46.2 us -> none  [the longest x1 35.3 us: radon_table(): sine = (jnp.sin(angle) * scale_r).astype(jnp.bfloat16)]
    neg x1 -> x0, other arithmetic: 32.3 us -> none  [radon_table(): second = jnp.stack([-sine, cosine], axis=2)]
    pallas_call x0 -> x3, Pallas kernels: none -> 23.8 us  [the longest x2 21.3 us: swap(): pl.pallas_call(functools.partial(swap_kernel, sizes, ids is not None), ou...]
    dot_general x7 -> x4, matrix products: 30.3 us -> 8.65 us  [the longest x1 3.01 us: on_device(): lax.dot_general(clean, dft, (((1,), (1,)), ((), ())), preferred_element_t...]
    another operation x3 -> x0, other arithmetic: 16.2 us -> none  [the longest x1 13.3 us: radon_table(): return jnp.stack([first, second], axis=1)]
    all_to_all x1 -> x0, blocking collectives: 14.9 us -> none  [on_device(): lax.all_to_all(back_rows, ('mid', 'freq'), split_axis=0, concat_axis=0, t...]
    all_to_all x2 -> x0, starting transfers between devices: 13.3 us -> none  [the longest x1 7.28 us: on_device(): lax.all_to_all(flat_cells, ('mid', 'freq'), split_axis=0, concat_axis=0,...]
    reduce_scatter x1 -> x0, waiting for transfers between devices: 8.35 us -> none  [on_device(): lax.psum_scatter(model_part, 'off', scatter_dimension=1, tiled=True)]
  transfers between devices with their start and end apart: 5 -> 0, of which waited for: 1 -> 0; matrix products, arithmetic and copies ran while one was open for 51% -> 0% of each run, Pallas kernels for 0% -> 0%
where the time goes in v2:
time: 40.5 us; the launch traced here: 40.2 us
  Pallas kernels  23.9 us (59%)
  matrix products  8.65 us (21%)
  local copies, waits for them, and re-layouts  6.28 us (16%)
  other arithmetic  1.28 us (3%)
    pallas_call x2, Pallas kernels, swap(): pl.pallas_call(functools.partial(swap_kernel, sizes, ids is not None), ou...  21.3 us
    dot_general x1, matrix products, on_device(): lax.dot_general(clean, dft, (((1,), (1,)), ((), ())), preferred_element_t...  3.01 us
    pallas_call x1, Pallas kernels, radon(): pl.pallas_call(functools.partial(radon_kernel, n_mid, n_off), out_shape=j...  2.56 us
    dot_general x1, matrix products, on_device(): spectra = jnp.dot(filtered, dft, preferred_element_type=f32).astype(bf16)  2.52 us
    dot_general x1, matrix products, on_device(): lax.dot_general(rows, mix, (((0,), (0,)), ((), ())), preferred_element_ty...  2.12 us
    convert_element_type x3, local copies, waits for them, and re-layouts, on_device(): clean = (spectra.astype(f32) - own_mult.astype(f32)).astype(bf16)  1.7 us
    add x1, other arithmetic, on_device(): rows, ids = swap(blocks, sizes, 0, midpoint_of * NOFF + offset_of)  1.28 us
    reshape x2, local copies, waits for them, and re-layouts, on_device(): rows = rows.reshape(total, tr_dev // pack, pack, width)  1.08 us

profile of v2, /device:TPU:0, one launch (start us, length us, event | category | flops | bytes accessed | tf_op | source)
XLA Modules:
  0.0 40.2 jit_solution(14322803185907440534)
XLA Ops:
  0.0 0.0 copy-start
  0.0 0.9 %dynamic_slice.3 = f32[32]{0:T(128)S(1)} dynamic-slice(f32[256]{0:T(256)} %param.11, s32[]{:T(128)S(6)} %select_n.13), dynamic_slice_sizes={32} | dynamic-slice | bytes 260 | tf_op jit(solution)/shard_map/dynamic_slice | solution.py:208
  0.9 1.3 %multiply_add_fusion.refs_1_ = s32[1,512]{1,0:T(1,128)} fusion(s32[1,512]{1,0:T(1,128)} %param.10, s32[1,512]{1,0:T(1,128)} %param.9), kind=kLoop, calls=%fused_computation.21 | loop fusion | flops 1024 | bytes 6144 | tf_op jit(solution)/shard_map/add | solution.py:191
  2.2 0.1 broadcast_in_dim.25.level
  2.3 0.0 copy-done
  2.3 2.5 %convolution_convert_fusion = bf16[64,1024]{1,0:T(8,128)(2,1)S(1)} fusion(bf16[1024,1024]{1,0:T(8,128)(2,1)} %constant.33.clone, bf16[1024,1024]{1,0:T(8,128)(2,1)S(1)} %copy-done, bf16[1,64,1024]{2,1,0:T(8,128)(2,1)} %param.7), kind=kOutput, calls=%fused_computation.11 | convolution fusion | flops 268566528 | bytes 4456448 | tf_op jit(solution)/shard_map/dot_general | solution.py:188
  4.8 0.2 reshape.34
  5.0 0.3 copy.23
  5.3 0.8 %reshape.35.refs_0_ = bf16[16,32,128]{2,1,0:T(8,128)(2,1)} reshape(bf16[16,32,2,64]{3,2,1,0:T(2,128)(2,1)S(1)} %bitcast.35) | data formatting | bytes 262144 | tf_op jit(solution)/shard_map/reshape | solution.py:190
  6.1 11.9 %shard_map.73 = (bf16[16,32,128]{2,1,0:T(8,128)(2,1)}, s32[2,1,512]{2,1,0:T(1,128)}) custom-call(bf16[16,32,128]{2,1,0:T(8,128)(2,1)} %reshape.35.refs_0_, s32[1,512]{1,0:T(1,128)} %multiply_add_fusion.refs_1_), custom_call_target="tpu_custom_call" | custom-call | tf_op jit(solution)/shard_map/pallas_call | solution.py:126
  18.0 1.0 %reshape.36 = bf16[16,32,2,64]{3,2,1,0:T(2,128)(2,1)S(1)} reshape(bf16[16,32,128]{2,1,0:T(8,128)(2,1)} %get-tuple-element.8) | data formatting | bytes 262144 | tf_op jit(solution)/shard_map/reshape | solution.py:192
  19.1 2.1 %fusion.9 = bf16[8,8,8,128]{3,1,2,0:T(8,128)(2,1)S(1)} fusion(bf16[1024,64]{1,0:T(8,128)(2,1)S(1)} %bitcast.37, s32[1024]{0:T(1024)} %bitcast.38), kind=kOutput, calls=%fused_computation.15 | convolution fusion | flops 141623296 | bytes 266240 | tf_op jit(solution)/shard_map/dot_general | solution.py:201
  21.2 0.0 copy-start.1
  21.2 2.6 %shard_map.74 = bf16[2,32,8,128]{3,2,1,0:T(8,128)(2,1)S(1)} custom-call(bf16[2,32,8,128]{3,2,1,0:T(8,128)(2,1)S(1)} %bitcast.32, f32[32,1,128]{2,1,0:T(1,128)S(1)} %broadcast_in_dim.25.level, bf16[512,256,128]{2,1,0:T(8,128)(2,1)} %constant.34.clone.table), custom_call_target="tpu_custom_call" | custom-call | tf_op jit(solution)/shard_map/pallas_call | solution.py:161
  23.8 0.0 copy-done.1
  23.8 1.0 %fusion.6 = bf16[1024,64]{0,1:T(8,128)(2,1)S(1)} fusion(s32[1024]{0:T(1024)S(1)} %bitcast.39, bf16[8,8,8,128]{3,2,1,0:T(8,128)(2,1)S(1)} %bitcast.33), kind=kOutput, calls=%fused_computation.10 | convolution fusion | flops 135331840 | bytes 266240 | tf_op jit(solution)/shard_map/dot_general | solution.py:213
  24.8 0.2 copy.13
  25.0 0.2 copy.14
  25.3 0.8 %reshape.41.refs_0_ = bf16[16,32,128]{2,1,0:T(8,128)(2,1)} reshape(bf16[16,32,2,64]{3,2,1,0:T(2,128)(2,1)S(1)} %copy.14) | data formatting | bytes 262144 | tf_op jit(solution)/shard_map/reshape | solution.py:217
  26.1 9.4 %shard_map.75 = bf16[16,32,128]{2,1,0:T(8,128)(2,1)} custom-call(bf16[16,32,128]{2,1,0:T(8,128)(2,1)} %reshape.41.refs_0_), custom_call_target="tpu_custom_call" | custom-call | tf_op jit(solution)/shard_map/pallas_call | solution.py:126
  35.5 1.2 %reshape.43 = f32[16,32,2,64]{3,2,1,0:T(2,128)S(1)} reshape(bf16[16,32,128]{2,1,0:T(8,128)(2,1)} %shard_map.75) | data formatting | bytes 393216 | tf_op jit(solution)/shard_map/convert_element_type | solution.py:221
  36.7 0.3 copy.15
  37.0 0.2 reshape.42
  37.2 3.0 %fusion.8 = bf16[1,64,1024]{2,1,0:T(8,128)(2,1)} fusion(bf16[1024,1024]{1,0:T(8,128)(2,1)} %constant.33.clone, f32[64,1024]{1,0:T(8,128)S(1)} %reshape.42, bf16[64,1024]{1,0:T(8,128)(2,1)S(1)} %convolution_convert_fusion), kind=kOutput, calls=%fused_computation.14 | convolution fusion | flops 134545408 | bytes 2621440 | tf_op jit(solution)/shard_map/dot_general | solution.py:222
  (2 shorter events, 0.1 us)
Async XLA Ops:
  0.0 2.3 %copy-start = (bf16[1024,1024]{1,0:T(8,128)(2,1)S(1)}, bf16[1024,1024]{1,0:T(8,128)(2,1)}, u32[]{:S(2)}) copy-start(bf16[1024,1024]{1,0:T(8,128)(2,1)} %param.8) | copy-start | bytes 6291460
  21.2 2.6 %copy-start.1 = (s32[2,1,512]{2,1,0:T(1,128)S(1)}, s32[2,1,512]{2,1,0:T(1,128)}, u32[]{:S(2)}) copy-start(s32[2,1,512]{2,1,0:T(1,128)} %get-tuple-element.7) | copy-start | bytes 12292

commit v3 on v2

--- a/solution.py
+++ b/solution.py
@@ -168,6 +168,147 @@
     )(smooth, level, table)
 
 
+def fused_kernel(sizes, pack, blocks, ids, level, table, ret, got, got_ids, back, weights, near, same, cube, t_sem, own_sem, send_sem, recv_sem, id_own, id_send, id_recv):
+    index, total, ahead = place(sizes)
+    n_off, n_mid, n_freq = sizes
+    off = lax.axis_index("off")
+    f32, bf16 = jnp.float32, jnp.bfloat16
+    width, mids = cube.shape[:2]
+    count = width // 2
+    n_cells = mids * NOFF
+    per_half = ids.shape[1]
+    barrier = pltpu.get_barrier_semaphore()
+
+    @pl.loop(1, total)
+    def _(i):
+        signal(barrier, **ahead(i)[1])
+
+    q = (lax.axis_index("freq") * n_mid + lax.axis_index("mid")) * n_off + off
+    fetch = pltpu.make_async_copy(table.at[pl.ds(q * count, count)], weights, t_sem)
+    fetch.start()
+    own = pltpu.make_async_copy(blocks.at[index], got.at[index], own_sem.at[0])
+    own.start()
+    own_ids = pltpu.make_async_copy(ids, got_ids.at[off], id_own)
+    own_ids.start()
+    pl.semaphore_wait(barrier, total - 1)
+
+    def block_copy(way, src, dst, i):
+        there, device = ahead(i)
+        return send(src.at[there], dst.at[index], send_sem.at[way, i], recv_sem.at[way, i], **device)
+
+    def id_copy(d):
+        return send(ids, got_ids.at[off], id_send.at[d], id_recv.at[d], off=(off + d) % n_off)
+
+    for d in range(1, n_off):
+        id_copy(d).start()
+
+    @pl.loop(1, total)
+    def _(i):
+        block_copy(0, blocks, got, i).start()
+
+    own_ids.wait()
+    for d in range(1, n_off):
+        id_copy(d).wait()
+    step = 128
+
+    @pl.loop(0, n_cells // step)
+    def _(j):
+        here = pl.multiple_of(j * step, step)
+        cell = lax.broadcasted_iota(jnp.int32, (step, per_half), 0) + here
+        for o in range(n_off):
+            for pk in range(pack):
+                away = jnp.abs(cell - got_ids[o, pl.ds(pk, 1), :])
+                hit = jnp.where(away == 0, 1.0, 0.0)
+                near[pk, o, pl.ds(here, step)] = (0.5 * hit + jnp.where(away == NOFF, 0.25, 0.0)).astype(bf16)
+                same[pk, o, pl.ds(here, step)] = hit.astype(bf16)
+
+    own.wait()
+
+    @pl.loop(1, total)
+    def _(i):
+        block_copy(0, blocks, got, i).wait()
+
+    rows = jnp.transpose(got[...].reshape(n_off * per_half, pack * width).astype(f32)).astype(bf16)
+    smooth = jnp.zeros((width, n_cells), f32)
+    for pk in range(pack):
+        for o in range(n_off):
+            smooth += lax.dot_general(
+                rows[pk * width : (pk + 1) * width, o * per_half : (o + 1) * per_half],
+                near[pk, o],
+                (((1,), (1,)), ((), ())),
+                preferred_element_type=f32,
+            )
+    for c in range(mids):
+        cube[:, c, :] = smooth[:, c * NOFF : (c + 1) * NOFF]
+    re, im = cube[pl.ds(0, count)], cube[pl.ds(count, count)]
+    first = jnp.concatenate([re, -im], axis=2)
+    second = jnp.concatenate([im, re], axis=2)
+    x = jnp.concatenate([first, second], axis=1).astype(bf16)
+    fetch.wait()
+    model = lax.dot_general(x, weights[...], (((2,), (1,)), ((0,), (0,))), preferred_element_type=f32)
+    model_re, model_im = model[:, :mids], model[:, mids:]
+    power = model_re * model_re + model_im * model_im
+    keep = (lax.broadcasted_iota(jnp.int32, power.shape, 2) >= NP // 4).astype(f32)
+    lev = level[...]
+    factor = power / (power + lev * lev) * keep
+    kept = jnp.concatenate([model_re * factor, model_im * factor], axis=1).astype(bf16)
+    both = lax.dot_general(kept, weights[...], (((2,), (2,)), ((0,), (0,))), preferred_element_type=f32)
+    cube[pl.ds(0, count)] = both[:, :mids, :NOFF] + both[:, mids:, NOFF:]
+    cube[pl.ds(count, count)] = both[:, mids:, :NOFF] - both[:, :mids, NOFF:]
+    mult = jnp.concatenate([cube[:, c, :] for c in range(mids)], axis=1).astype(bf16)
+    for o in range(n_off):
+        lines = [jnp.dot(mult, same[pk, o], preferred_element_type=f32) for pk in range(pack)]
+        lines = jnp.transpose(jnp.concatenate(lines, axis=0)).astype(bf16)
+        part = total // n_off
+        back[pl.ds(o * part, part)] = lines.reshape((part,) + blocks.shape[1:])
+    own_back = pltpu.make_async_copy(back.at[index], ret.at[index], own_sem.at[1])
+    own_back.start()
+
+    @pl.loop(1, total)
+    def _(i):
+        block_copy(1, back, ret, i).start()
+
+    own_back.wait()
+
+    @pl.loop(1, total)
+    def _(i):
+        block_copy(1, back, ret, i).wait()
+
+
+def fused(blocks, ids, level, table, sizes, pack):
+    total, n_off = blocks.shape[0], sizes[0]
+    count = level.shape[0]
+    per_half = ids.shape[1]
+    n_cells = n_off * per_half * pack
+    dma = pltpu.SemaphoreType.DMA
+    bf16 = jnp.bfloat16
+    return pl.pallas_call(
+        functools.partial(fused_kernel, sizes, pack),
+        out_shape=jax.ShapeDtypeStruct(blocks.shape, blocks.dtype),
+        in_specs=[VMEM, VMEM, VMEM, ANY],
+        out_specs=VMEM,
+        scratch_shapes=[
+            pltpu.VMEM(blocks.shape, bf16),
+            pltpu.VMEM((n_off,) + ids.shape, jnp.int32),
+            pltpu.VMEM(blocks.shape, bf16),
+            pltpu.VMEM((count, 2 * NOFF, NP), bf16),
+            pltpu.VMEM((pack, n_off, n_cells, per_half), bf16),
+            pltpu.VMEM((pack, n_off, n_cells, per_half), bf16),
+            pltpu.VMEM((2 * count, n_cells // NOFF, NOFF), jnp.float32),
+            dma,
+            dma((2,)),
+            dma((2, total)),
+            dma((2, total)),
+            dma,
+            dma((n_off,)),
+            dma((n_off,)),
+        ],
+        compiler_params=pltpu.CompilerParams(
+            collective_id=2, has_side_effects=True, vmem_limit_bytes=40 * 1024 * 1024
+        ),
+    )(blocks, ids, level, table)
+
+
 def on_device(dft, weights, traces, time_filter, midpoint_of, offset_of, shrink_level):
     n_mid = lax.axis_size("mid")
     n_freq = lax.axis_size("freq")
@@ -188,34 +329,25 @@
     spectra = jnp.dot(filtered, dft, preferred_element_type=f32).astype(bf16)
     blocks = spectra.reshape(pack, tr_dev // pack, total, width)
     blocks = jnp.transpose(blocks, (2, 1, 0, 3)).reshape(total, tr_dev // pack, pack * width)
-    rows, ids = swap(blocks, sizes, 0, midpoint_of * NOFF + offset_of)
-    rows = rows.reshape(total, tr_dev // pack, pack, width)
-    rows = jnp.transpose(rows, (0, 2, 1, 3)).reshape(n_traces, width)
-    cell_of = ids.reshape(n_traces)
-
-    small = n_traces <= 4096
-    if small:
-        cells = jnp.arange(n_traces, dtype=jnp.int32)[None, :]
-        away = jnp.abs(cell_of[:, None] - cells)
-        mix = jnp.where(away == 0, 0.5, jnp.where(away == NOFF, 0.25, 0.0)).astype(bf16)
-        smooth = lax.dot_general(rows, mix, (((0,), (0,)), ((), ())), preferred_element_type=f32)
-        smooth = smooth.astype(bf16).reshape(2, count, n_mids, NOFF)
+    own_levels = lax.dynamic_slice_in_dim(shrink_level, (me_mid * n_off + me_off) * count, count)
+    level = jnp.broadcast_to(own_levels[:, None, None], (count, 1, NP))
+    own_ids = midpoint_of * NOFF + offset_of
+    if n_traces <= 4096:
+        own_ids = jnp.transpose(own_ids.reshape(total // n_off, pack, tr_dev // pack), (1, 0, 2)).reshape(pack, -1)
+        returned = fused(blocks, own_ids, level, weights, sizes, pack)
     else:
+        rows, ids = swap(blocks, sizes, 0, own_ids)
+        rows = rows.reshape(total, tr_dev // pack, pack, width)
+        rows = jnp.transpose(rows, (0, 2, 1, 3)).reshape(n_traces, width)
+        cell_of = ids.reshape(n_traces)
         gather = jnp.zeros((n_traces, width), bf16).at[cell_of].set(rows)
         edged = jnp.pad(gather.reshape(n_mids, NOFF, 2, count).astype(f32), ((1, 1), (0, 0), (0, 0), (0, 0)))
         smooth = ((edged[:-2] + 2.0 * edged[1:-1] + edged[2:]) * 0.25).astype(bf16)
         smooth = jnp.transpose(smooth, (2, 3, 0, 1))
-    own_levels = lax.dynamic_slice_in_dim(shrink_level, (me_mid * n_off + me_off) * count, count)
-    level = jnp.broadcast_to(own_levels[:, None, None], (count, 1, NP))
-    mult = radon(smooth, level, weights, n_mid, n_off).reshape(width, n_traces)
-    if small:
-        pick = (cell_of[:, None] == cells).astype(bf16)
-        back = lax.dot_general(pick, mult, (((1,), (1,)), ((), ())), preferred_element_type=f32).astype(bf16)
-    else:
-        back = jnp.transpose(mult)[cell_of]
-    back = back.reshape(total, pack, tr_dev // pack, width)
-    back = jnp.transpose(back, (0, 2, 1, 3)).reshape(total, tr_dev // pack, pack * width)
-    (returned,) = swap(back, sizes, 1)
+        mult = radon(smooth, level, weights, n_mid, n_off).reshape(width, n_traces)
+        back = jnp.transpose(mult)[cell_of].reshape(total, pack, tr_dev // pack, width)
+        back = jnp.transpose(back, (0, 2, 1, 3)).reshape(total, tr_dev // pack, pack * width)
+        (returned,) = swap(back, sizes, 1)
     returned = returned.reshape(total, tr_dev // pack, pack, width)
     own_mult = jnp.transpose(returned, (2, 1, 0, 3)).reshape(tr_dev, total * width)
     clean = (spectra.astype(f32) - own_mult.astype(f32)).astype(bf16)

time: 40.5 us -> 28.5 us (0.70)
  Pallas kernels: 23.9 us -> 19.1 us
  local copies, waits for them, and re-layouts: 6.28 us -> 2.83 us
  matrix products: 8.65 us -> 5.53 us
  other arithmetic: 1.28 us -> 0.72 us
    pallas_call x3 -> x1, Pallas kernels: 23.8 us -> 19.1 us  [fused(): pl.pallas_call(functools.partial(fused_kernel, sizes, pack), out_shape=ja...]
    dot_general x2 -> x0, matrix products: 3.12 us -> none  [the longest x1 2.12 us: on_device(): lax.dot_general(rows, mix, (((0,), (0,)), ((), ())), preferred_element_ty...]
    reshape x3, local copies, waits for them, and re-layouts: 1.89 us -> 0.17 us  [the longest x2 0.09 us: on_device(): own_ids.reshape(total // n_off, pack, tr_dev // pack)]
    convert_element_type x3, local copies, waits for them, and re-layouts: 1.7 us -> 0.79 us  [on_device(): clean = (spectra.astype(f32) - own_mult.astype(f32)).astype(bf16)]
    reshape x1, local copies, waits for them, and re-layouts: 0.81 us -> 0.14 us  [on_device(): jnp.transpose(blocks, (2, 1, 0, 3))]
    add x1, other arithmetic: 1.28 us -> 0.72 us  [on_device(): own_ids = midpoint_of * NOFF + offset_of]
where the time goes in v3:
time: 28.5 us; the launch traced here: 28.3 us
  Pallas kernels  19.1 us (67%)
  matrix products  5.53 us (19%)
  local copies, waits for them, and re-layouts  2.83 us (10%)
  other arithmetic  0.72 us (3%)
    pallas_call x1, Pallas kernels, fused(): pl.pallas_call(functools.partial(fused_kernel, sizes, pack), out_shape=ja...  19.1 us
    dot_general x1, matrix products, on_device(): lax.dot_general(clean, dft, (((1,), (1,)), ((), ())), preferred_element_t...  3.01 us
    dot_general x1, matrix products, on_device(): spectra = jnp.dot(filtered, dft, preferred_element_type=f32).astype(bf16)  2.52 us
    dynamic_slice x1, local copies, waits for them, and re-layouts, on_device(): lax.dynamic_slice_in_dim(shrink_level, (me_mid * n_off + me_off) * count,...  0.9 us
    convert_element_type x3, local copies, waits for them, and re-layouts, on_device(): clean = (spectra.astype(f32) - own_mult.astype(f32)).astype(bf16)  0.79 us
    add x1, other arithmetic, on_device(): own_ids = midpoint_of * NOFF + offset_of  0.72 us

profile of v3, /device:TPU:0, one launch (start us, length us, event | category | flops | bytes accessed | tf_op | source)
XLA Modules:
  0.0 28.3 jit_solution(3548559061326493326)
XLA Ops:
  0.0 0.0 copy-start
  0.0 0.9 %dynamic_slice.3 = f32[32]{0:T(128)S(1)} dynamic-slice(f32[256]{0:T(256)} %param.11, s32[]{:T(128)S(6)} %select_n.3), dynamic_slice_sizes={32} | dynamic-slice | bytes 260 | tf_op jit(solution)/shard_map/dynamic_slice | solution.py:332
  0.9 0.7 %add_reduce_fusion = s32[512]{0:T(512)S(1)} fusion(s32[1,512]{1,0:T(1,128)} %param.10, s32[1,512]{1,0:T(1,128)} %param.9), kind=kLoop, calls=%fused_computation.9 | loop fusion | flops 1024 | bytes 6144 | tf_op jit(solution)/shard_map/add | solution.py:334
  1.6 0.1 reshape.23
  1.7 0.1 reshape.24.ids
  1.8 0.1 broadcast_in_dim.4.level
  1.9 0.0 copy-done
  1.9 2.5 %convolution_convert_fusion = bf16[64,1024]{1,0:T(8,128)(2,1)S(1)} fusion(bf16[1024,1024]{1,0:T(8,128)(2,1)} %constant.25.clone, bf16[1024,1024]{1,0:T(8,128)(2,1)S(1)} %copy-done, bf16[1,64,1024]{2,1,0:T(8,128)(2,1)} %param.7), kind=kOutput, calls=%fused_computation.2 | convolution fusion | flops 268566528 | bytes 4456448 | tf_op jit(solution)/shard_map/dot_general | solution.py:329
  4.4 0.0 copy-start.1
  4.4 0.2 reshape.21
  4.6 0.3 copy.13
  4.9 0.2 copy-done.1
  5.1 0.1 reshape.22.blocks
  5.2 19.1 %shard_map.73 = bf16[16,32,128]{2,1,0:T(8,128)(2,1)S(1)} custom-call(bf16[16,32,128]{2,1,0:T(8,128)(2,1)S(1)} %reshape.22.blocks, s32[2,256]{1,0:T(2,128)S(1)} %reshape.24.ids, f32[32,1,128]{2,1,0:T(1,128)S(1)} %broadcast_in_dim.4.level, bf16[512,256,128]{2,1,0:T(8,128)(2,1)} %constant.26.clone.table), custom_call_target="tpu_custom_call" | custom-call | tf_op jit(solution)/shard_map/pallas_call | solution.py:285
  24.4 0.0 copy-start.2
  24.4 0.3 %reshape.26 = f32[16,32,2,64]{3,2,1,0:T(2,128)S(1)} reshape(bf16[16,32,128]{2,1,0:T(8,128)(2,1)S(1)} %shard_map.73) | data formatting | bytes 393216 | tf_op jit(solution)/shard_map/convert_element_type | solution.py:353
  24.7 0.3 %copy.10 = f32[2,32,16,64]{3,2,1,0:T(8,128)S(1)} copy(f32[2,32,16,64]{3,0,1,2:T(2,128)S(1)} %bitcast.18) | data formatting | bytes 524288 | tf_op jit(solution)/shard_map/convert_element_type | solution.py:353
  25.0 0.2 reshape.25
  25.2 0.1 copy-done.2
  25.3 3.0 %fusion.1 = bf16[1,64,1024]{2,1,0:T(8,128)(2,1)} fusion(bf16[1024,1024]{1,0:T(8,128)(2,1)} %constant.25.clone, f32[64,1024]{1,0:T(8,128)S(1)} %reshape.25, bf16[64,1024]{1,0:T(8,128)(2,1)S(1)} %copy-done.2), kind=kOutput, calls=%fused_computation.4 | convolution fusion | flops 134545408 | bytes 2621440 | tf_op jit(solution)/shard_map/dot_general | solution.py:354
  (1 shorter events, 0.0 us)
Async XLA Ops:
  0.0 1.9 %copy-start = (bf16[1024,1024]{1,0:T(8,128)(2,1)S(1)}, bf16[1024,1024]{1,0:T(8,128)(2,1)}, u32[]{:S(2)}) copy-start(bf16[1024,1024]{1,0:T(8,128)(2,1)} %param.8) | copy-start | bytes 6291460
  4.4 0.7 %copy-start.1 = (bf16[64,1024]{1,0:T(8,128)(2,1)}, bf16[64,1024]{1,0:T(8,128)(2,1)S(1)}, u32[]{:S(2)}) copy-start(bf16[64,1024]{1,0:T(8,128)(2,1)S(1)} %convolution_convert_fusion) | copy-start | bytes 393220
  24.4 0.9 %copy-start.2 = (bf16[64,1024]{1,0:T(8,128)(2,1)S(1)}, bf16[64,1024]{1,0:T(8,128)(2,1)}, u32[]{:S(2)}) copy-start(bf16[64,1024]{1,0:T(8,128)(2,1)} %copy-done.1) | copy-start | bytes 393220

commit v4 on v3

--- a/solution.py
+++ b/solution.py
@@ -168,7 +168,7 @@
     )(smooth, level, table)
 
 
-def fused_kernel(sizes, pack, blocks, ids, level, table, ret, got, got_ids, back, weights, near, same, cube, t_sem, own_sem, send_sem, recv_sem, id_own, id_send, id_recv):
+def fused_kernel(sizes, pack, traces, time_filter, ids, level, dft_hbm, table, out, dft, spec, blocks, ret, f_sem, got, got_ids, back, weights, near, same, cube, t_sem, own_sem, send_sem, recv_sem, id_own, id_send, id_recv):
     index, total, ahead = place(sizes)
     n_off, n_mid, n_freq = sizes
     off = lax.axis_index("off")
@@ -185,11 +185,21 @@
 
     q = (lax.axis_index("freq") * n_mid + lax.axis_index("mid")) * n_off + off
     fetch = pltpu.make_async_copy(table.at[pl.ds(q * count, count)], weights, t_sem)
+    fetch_dft = pltpu.make_async_copy(dft_hbm, dft, f_sem)
+    fetch_dft.start()
     fetch.start()
+    own_ids = pltpu.make_async_copy(ids, got_ids.at[off], id_own)
+    own_ids.start()
+    filtered = jnp.dot(traces[...], time_filter[...], preferred_element_type=f32).astype(bf16)
+    fetch_dft.wait()
+    spectra = jnp.dot(filtered, dft[...], preferred_element_type=f32).astype(bf16)
+    spec[...] = spectra
+    lines = blocks.shape[1]
+    for d in range(total):
+        parts = [spectra[pk * lines : (pk + 1) * lines, d * width : (d + 1) * width] for pk in range(pack)]
+        blocks[d] = jnp.concatenate(parts, axis=1)
     own = pltpu.make_async_copy(blocks.at[index], got.at[index], own_sem.at[0])
     own.start()
-    own_ids = pltpu.make_async_copy(ids, got_ids.at[off], id_own)
-    own_ids.start()
     pl.semaphore_wait(barrier, total - 1)
 
     def block_copy(way, src, dst, i):
@@ -249,7 +259,8 @@
     model_re, model_im = model[:, :mids], model[:, mids:]
     power = model_re * model_re + model_im * model_im
     keep = (lax.broadcasted_iota(jnp.int32, power.shape, 2) >= NP // 4).astype(f32)
-    lev = level[...]
+    own_level = level[lax.axis_index("mid") * n_off + off]
+    lev = jnp.transpose(jnp.broadcast_to(own_level, (NP, count)))[:, None, :]
     factor = power / (power + lev * lev) * keep
     kept = jnp.concatenate([model_re * factor, model_im * factor], axis=1).astype(bf16)
     both = lax.dot_general(kept, weights[...], (((2,), (2,)), ((0,), (0,))), preferred_element_type=f32)
@@ -257,10 +268,10 @@
     cube[pl.ds(count, count)] = both[:, mids:, :NOFF] - both[:, :mids, NOFF:]
     mult = jnp.concatenate([cube[:, c, :] for c in range(mids)], axis=1).astype(bf16)
     for o in range(n_off):
-        lines = [jnp.dot(mult, same[pk, o], preferred_element_type=f32) for pk in range(pack)]
-        lines = jnp.transpose(jnp.concatenate(lines, axis=0)).astype(bf16)
+        routed = [jnp.dot(mult, same[pk, o], preferred_element_type=f32) for pk in range(pack)]
+        routed = jnp.transpose(jnp.concatenate(routed, axis=0)).astype(bf16)
         part = total // n_off
-        back[pl.ds(o * part, part)] = lines.reshape((part,) + blocks.shape[1:])
+        back[pl.ds(o * part, part)] = routed.reshape((part,) + blocks.shape[1:])
     own_back = pltpu.make_async_copy(back.at[index], ret.at[index], own_sem.at[1])
     own_back.start()
 
@@ -274,23 +285,41 @@
     def _(i):
         block_copy(1, back, ret, i).wait()
 
-
-def fused(blocks, ids, level, table, sizes, pack):
-    total, n_off = blocks.shape[0], sizes[0]
-    count = level.shape[0]
+    own_mult = jnp.concatenate(
+        [
+            jnp.concatenate([ret[d][:, pk * width : (pk + 1) * width] for d in range(total)], axis=1)
+            for pk in range(pack)
+        ],
+        axis=0,
+    )
+    clean = (spec[...].astype(f32) - own_mult.astype(f32)).astype(bf16)
+    sums = lax.dot_general(clean, dft[...], (((1,), (1,)), ((), ())), preferred_element_type=f32)
+    out[...] = (2.0 * sums).astype(bf16)
+
+
+def fused(traces, time_filter, ids, level, dft, table, sizes, pack):
+    n_off = sizes[0]
+    total = n_off * sizes[1] * sizes[2]
+    count = level.shape[2]
+    shape = (total, traces.shape[0] // pack, pack * 2 * count)
     per_half = ids.shape[1]
     n_cells = n_off * per_half * pack
     dma = pltpu.SemaphoreType.DMA
     bf16 = jnp.bfloat16
     return pl.pallas_call(
         functools.partial(fused_kernel, sizes, pack),
-        out_shape=jax.ShapeDtypeStruct(blocks.shape, blocks.dtype),
-        in_specs=[VMEM, VMEM, VMEM, ANY],
+        out_shape=jax.ShapeDtypeStruct(traces.shape, traces.dtype),
+        in_specs=[VMEM, VMEM, VMEM, VMEM, ANY, ANY],
         out_specs=VMEM,
         scratch_shapes=[
-            pltpu.VMEM(blocks.shape, bf16),
+            pltpu.VMEM(dft.shape, bf16),
+            pltpu.VMEM((traces.shape[0], dft.shape[1]), bf16),
+            pltpu.VMEM(shape, bf16),
+            pltpu.VMEM(shape, bf16),
+            dma,
+            pltpu.VMEM(shape, bf16),
             pltpu.VMEM((n_off,) + ids.shape, jnp.int32),
-            pltpu.VMEM(blocks.shape, bf16),
+            pltpu.VMEM(shape, bf16),
             pltpu.VMEM((count, 2 * NOFF, NP), bf16),
             pltpu.VMEM((pack, n_off, n_cells, per_half), bf16),
             pltpu.VMEM((pack, n_off, n_cells, per_half), bf16),
@@ -306,7 +335,7 @@
         compiler_params=pltpu.CompilerParams(
             collective_id=2, has_side_effects=True, vmem_limit_bytes=40 * 1024 * 1024
         ),
-    )(blocks, ids, level, table)
+    )(traces, time_filter, ids, level, dft, table)
 
 
 def on_device(dft, weights, traces, time_filter, midpoint_of, offset_of, shrink_level):
@@ -325,29 +354,29 @@
     n_mids = n_traces // NOFF
     f32, bf16 = jnp.float32, jnp.bfloat16
 
+    own_ids = midpoint_of * NOFF + offset_of
+    if n_traces <= 4096:
+        own_ids = jnp.transpose(own_ids.reshape(total // n_off, pack, tr_dev // pack), (1, 0, 2)).reshape(pack, -1)
+        level = shrink_level.reshape(n_mid * n_off, 1, count)
+        return fused(traces[0], time_filter, own_ids, level, dft, weights, sizes, pack)[None]
     filtered = jnp.dot(traces[0], time_filter, preferred_element_type=f32).astype(bf16)
     spectra = jnp.dot(filtered, dft, preferred_element_type=f32).astype(bf16)
     blocks = spectra.reshape(pack, tr_dev // pack, total, width)
     blocks = jnp.transpose(blocks, (2, 1, 0, 3)).reshape(total, tr_dev // pack, pack * width)
     own_levels = lax.dynamic_slice_in_dim(shrink_level, (me_mid * n_off + me_off) * count, count)
     level = jnp.broadcast_to(own_levels[:, None, None], (count, 1, NP))
-    own_ids = midpoint_of * NOFF + offset_of
-    if n_traces <= 4096:
-        own_ids = jnp.transpose(own_ids.reshape(total // n_off, pack, tr_dev // pack), (1, 0, 2)).reshape(pack, -1)
-        returned = fused(blocks, own_ids, level, weights, sizes, pack)
-    else:
-        rows, ids = swap(blocks, sizes, 0, own_ids)
-        rows = rows.reshape(total, tr_dev // pack, pack, width)
-        rows = jnp.transpose(rows, (0, 2, 1, 3)).reshape(n_traces, width)
-        cell_of = ids.reshape(n_traces)
-        gather = jnp.zeros((n_traces, width), bf16).at[cell_of].set(rows)
-        edged = jnp.pad(gather.reshape(n_mids, NOFF, 2, count).astype(f32), ((1, 1), (0, 0), (0, 0), (0, 0)))
-        smooth = ((edged[:-2] + 2.0 * edged[1:-1] + edged[2:]) * 0.25).astype(bf16)
-        smooth = jnp.transpose(smooth, (2, 3, 0, 1))
-        mult = radon(smooth, level, weights, n_mid, n_off).reshape(width, n_traces)
-        back = jnp.transpose(mult)[cell_of].reshape(total, pack, tr_dev // pack, width)
-        back = jnp.transpose(back, (0, 2, 1, 3)).reshape(total, tr_dev // pack, pack * width)
-        (returned,) = swap(back, sizes, 1)
+    rows, ids = swap(blocks, sizes, 0, own_ids)
+    rows = rows.reshape(total, tr_dev // pack, pack, width)
+    rows = jnp.transpose(rows, (0, 2, 1, 3)).reshape(n_traces, width)
+    cell_of = ids.reshape(n_traces)
+    gather = jnp.zeros((n_traces, width), bf16).at[cell_of].set(rows)
+    edged = jnp.pad(gather.reshape(n_mids, NOFF, 2, count).astype(f32), ((1, 1), (0, 0), (0, 0), (0, 0)))
+    smooth = ((edged[:-2] + 2.0 * edged[1:-1] + edged[2:]) * 0.25).astype(bf16)
+    smooth = jnp.transpose(smooth, (2, 3, 0, 1))
+    mult = radon(smooth, level, weights, n_mid, n_off).reshape(width, n_traces)
+    back = jnp.transpose(mult)[cell_of].reshape(total, pack, tr_dev // pack, width)
+    back = jnp.transpose(back, (0, 2, 1, 3)).reshape(total, tr_dev // pack, pack * width)
+    (returned,) = swap(back, sizes, 1)
     returned = returned.reshape(total, tr_dev // pack, pack, width)
     own_mult = jnp.transpose(returned, (2, 1, 0, 3)).reshape(tr_dev, total * width)
     clean = (spectra.astype(f32) - own_mult.astype(f32)).astype(bf16)

time: 28.5 us -> 26.5 us (0.930)
  matrix products: 5.53 us -> 0 us
  local copies, waits for them, and re-layouts: 2.83 us -> 5.68 us
  Pallas kernels: 19.1 us -> 19.8 us
    dot_general x2 -> x0, matrix products: 5.53 us -> none  [the longest x1 3.01 us: on_device(): lax.dot_general(clean, dft, (((1,), (1,)), ((), ())), preferred_element_t...]
    unnamed x6 -> x7, local copies, waits for them, and re-layouts: 0.28 us -> 4.74 us
    dynamic_slice x1 -> x0, local copies, waits for them, and re-layouts: 0.9 us -> none  [on_device(): lax.dynamic_slice_in_dim(shrink_level, (me_mid * n_off + me_off) * count,...]
    convert_element_type x3 -> x0, local copies, waits for them, and re-layouts: 0.79 us -> none  [on_device(): clean = (spectra.astype(f32) - own_mult.astype(f32)).astype(bf16)]
    pallas_call x1, Pallas kernels: 19.1 us -> 19.8 us  [fused(): pl.pallas_call(functools.partial(fused_kernel, sizes, pack), out_shape=ja...]
    reshape x3 -> x1, local copies, waits for them, and re-layouts: 0.59 us -> 0.76 us  [on_device(): level = shrink_level.reshape(n_mid * n_off, 1, count)]
where the time goes in v4:
time: 26.5 us; the launch traced here: 26.3 us
  Pallas kernels  19.8 us (75%)
  local copies, waits for them, and re-layouts  5.68 us (21%)
  other arithmetic  0.72 us (3%)
    pallas_call x1, Pallas kernels, fused(): pl.pallas_call(functools.partial(fused_kernel, sizes, pack), out_shape=ja...  19.8 us
    unnamed x7, local copies, waits for them, and re-layouts  4.74 us
    reshape x1, local copies, waits for them, and re-layouts, on_device(): level = shrink_level.reshape(n_mid * n_off, 1, count)  0.76 us
    add x1, other arithmetic, on_device(): own_ids = midpoint_of * NOFF + offset_of  0.72 us

profile of v4, /device:TPU:0, one launch (start us, length us, event | category | flops | bytes accessed | tf_op | source)
XLA Modules:
  0.0 26.3 jit_solution(7291626542768434216)
XLA Ops:
  0.0 0.7 %add_reduce_fusion = s32[512]{0:T(512)S(1)} fusion(s32[1,512]{1,0:T(1,128)} %param.10, s32[1,512]{1,0:T(1,128)} %param.9), kind=kLoop, calls=%fused_computation.1 | loop fusion | flops 1024 | bytes 6144 | tf_op jit(solution)/shard_map/add | solution.py:357
  0.7 0.8 %reshape.11.level = f32[8,1,32]{2,1,0:T(1,128)S(1)} reshape(f32[256]{0:T(256)} %param.11) | data formatting | bytes 2048 | tf_op jit(solution)/shard_map/reshape | solution.py:360
  1.5 0.1 reshape.9
  1.6 0.1 reshape.10.ids
  1.7 0.0 copy-start
  1.7 1.6 %copy-done = bf16[1024,1024]{1,0:T(8,128)(2,1)S(1)} copy-done((bf16[1024,1024]{1,0:T(8,128)(2,1)S(1)}, bf16[1024,1024]{1,0:T(8,128)(2,1)}, u32[]{:S(2)}) %copy-start) | copy-done | bytes 2097176
  3.2 0.0 copy-start.1
  3.2 1.6 %copy-done.1 = bf16[1024,1024]{1,0:T(8,128)(2,1)S(1)} copy-done((bf16[1024,1024]{1,0:T(8,128)(2,1)S(1)}, bf16[1024,1024]{1,0:T(8,128)(2,1)}, u32[]{:S(2)}) %copy-start.1) | copy-done | bytes 2097176
  4.8 0.0 copy-start.2
  4.8 0.9 %copy-done.2 = bf16[1,64,1024]{2,1,0:T(8,128)(2,1)S(1)} copy-done((bf16[1,64,1024]{2,1,0:T(8,128)(2,1)S(1)}, bf16[1,64,1024]{2,1,0:T(8,128)(2,1)}, u32[]{:S(2)}) %copy-start.2) | copy-done | bytes 131096
  5.7 19.8 %shard_map.73 = bf16[64,1024]{1,0:T(8,128)(2,1)S(1)} custom-call(bf16[64,1024]{1,0:T(8,128)(2,1)S(1)} %bitcast.6, bf16[1024,1024]{1,0:T(8,128)(2,1)S(1)} %copy-done, s32[2,256]{1,0:T(2,128)S(1)} %reshape.10.ids, f32[8,1,32]{2,1,0:T(1,128)S(1)} %reshape.11.level, bf16[1024,1024]{1,0:T(8,128)(2,1)S(1)} %copy-done.1, bf16[512,256,128]{2,1,0:T(8,128)(2,1)} %constant.7.clone.table), custom_call_target="tpu_custom_call" | custom-call | tf_op jit(solution)/shard_map/pallas_call | solution.py:309
  25.6 0.7 %copy.12 = bf16[1,64,1024]{2,1,0:T(8,128)(2,1)} copy(bf16[1,64,1024]{2,1,0:T(8,128)(2,1)S(1)} %bitcast.5) | data formatting | bytes 262144
  (1 shorter events, 0.0 us)
Async XLA Ops:
  1.7 1.6 %copy-start = (bf16[1024,1024]{1,0:T(8,128)(2,1)S(1)}, bf16[1024,1024]{1,0:T(8,128)(2,1)}, u32[]{:S(2)}) copy-start(bf16[1024,1024]{1,0:T(8,128)(2,1)} %time_filter.1) | copy-start | bytes 6291460
  3.2 1.6 %copy-start.1 = (bf16[1024,1024]{1,0:T(8,128)(2,1)S(1)}, bf16[1024,1024]{1,0:T(8,128)(2,1)}, u32[]{:S(2)}) copy-start(bf16[1024,1024]{1,0:T(8,128)(2,1)} %constant.6.clone.dft_hbm) | copy-start | bytes 6291460
  4.8 0.9 %copy-start.2 = (bf16[1,64,1024]{2,1,0:T(8,128)(2,1)S(1)}, bf16[1,64,1024]{2,1,0:T(8,128)(2,1)}, u32[]{:S(2)}) copy-start(bf16[1,64,1024]{2,1,0:T(8,128)(2,1)} %param.7) | copy-start | bytes 393220

commit v5 on v4

--- a/solution.py
+++ b/solution.py
@@ -333,7 +333,7 @@
             dma((n_off,)),
         ],
         compiler_params=pltpu.CompilerParams(
-            collective_id=2, has_side_effects=True, vmem_limit_bytes=40 * 1024 * 1024
+            collective_id=2, has_side_effects=True, vmem_limit_bytes=60 * 1024 * 1024
         ),
     )(traces, time_filter, ids, level, dft, table)
 

time: 26.5 us -> 26.7 us (level)
  Pallas kernels: 19.8 us -> 22.1 us
  local copies, waits for them, and re-layouts: 5.68 us -> 3.68 us
    unnamed x7 -> x1, local copies, waits for them, and re-layouts: 4.74 us -> 1.57 us
    pallas_call x1, Pallas kernels: 19.8 us -> 22.1 us  [fused(): pl.pallas_call(functools.partial(fused_kernel, sizes, pack), out_shape=ja...]
    reshape x1, local copies, waits for them, and re-layouts: 0.76 us -> 1.35 us  [on_device(): level = shrink_level.reshape(n_mid * n_off, 1, count)]
    reshape x1, local copies, waits for them, and re-layouts: 0.08 us -> 0.67 us  [on_device(): jnp.transpose(own_ids.reshape(total // n_off, pack, tr_dev // pack), (1,...]
where the time goes in v5:
time: 26.7 us; the launch traced here: 26.5 us
  Pallas kernels  22.1 us (83%)
  local copies, waits for them, and re-layouts  3.68 us (14%)
  other arithmetic  0.72 us (3%)
    pallas_call x1, Pallas kernels, fused(): pl.pallas_call(functools.partial(fused_kernel, sizes, pack), out_shape=ja...  22.1 us
    unnamed x1, local copies, waits for them, and re-layouts  1.57 us
    reshape x1, local copies, waits for them, and re-layouts, on_device(): level = shrink_level.reshape(n_mid * n_off, 1, count)  1.35 us
    add x1, other arithmetic, on_device(): own_ids = midpoint_of * NOFF + offset_of  0.72 us
    reshape x1, local copies, waits for them, and re-layouts, on_device(): jnp.transpose(own_ids.reshape(total // n_off, pack, tr_dev // pack), (1,...  0.67 us

profile of v5, /device:TPU:0, one launch (start us, length us, event | category | flops | bytes accessed | tf_op | source)
XLA Modules:
  0.0 26.5 jit_solution(27545999371442529)
XLA Ops:
  0.0 0.7 %add_reduce_fusion = s32[512]{0:T(512)S(1)} fusion(s32[1,512]{1,0:T(1,128)} %param.10, s32[1,512]{1,0:T(1,128)} %param.9), kind=kLoop, calls=%fused_computation.1 | loop fusion | flops 1024 | bytes 6144 | tf_op jit(solution)/shard_map/add | solution.py:357
  0.7 1.4 %reshape.11.level = f32[8,1,32]{2,1,0:T(1,128)} reshape(f32[256]{0:T(256)} %param.11) | data formatting | bytes 2048 | tf_op jit(solution)/shard_map/reshape | solution.py:360
  2.1 0.1 reshape.9
  2.2 0.7 %reshape.10.ids = s32[2,256]{1,0:T(2,128)} reshape(s32[2,8,32]{2,1,0:T(8,128)S(1)} %bitcast.7) | data formatting | bytes 4096 | tf_op jit(solution)/shard_map/reshape | solution.py:359
  2.8 22.1 %shard_map.73 = bf16[64,1024]{1,0:T(8,128)(2,1)} custom-call(bf16[64,1024]{1,0:T(8,128)(2,1)} %bitcast.6, bf16[1024,1024]{1,0:T(8,128)(2,1)} %time_filter.1, s32[2,256]{1,0:T(2,128)} %reshape.10.ids, f32[8,1,32]{2,1,0:T(1,128)} %reshape.11.level, bf16[1024,1024]{1,0:T(8,128)(2,1)} %constant.6.clone.dft_hbm, bf16[512,256,128]{2,1,0:T(8,128)(2,1)} %constant.7.clone.table), custom_call_target="tpu_custom_call" | custom-call | tf_op jit(solution)/shard_map/pallas_call | solution.py:309
  24.9 1.6 %copy.12 = bf16[1,64,1024]{2,1,0:T(8,128)(2,1)} copy(bf16[1,64,1024]{2,1,0:T(8,128)(2,1)} %bitcast.5) | data formatting | bytes 262144
  (1 shorter events, 0.0 us)
